TPU v7x, 256 devices: a whole 4x4x8 slice. The times are simulated.
256 devices in a mesh: ctx: 2 (over core), head: 4 (over x), doc: 32 (over z, y).
Axes of the slice: x: 4, y: 4, z: 8, core: 2. Of those that a mesh axis runs over, the one named last changes fastest.
Arguments:
- queries: bfloat16 [32, 256, 8192], P('doc', 'ctx', 'head'), may hold values from -360 to 360
- keys: bfloat16 [32, 8192, 1024], P('doc', 'ctx', 'head'), may hold values from -6 to 6
- values: bfloat16 [32, 8192, 1024], P('doc', 'ctx', 'head'), may hold values from -6 to 6
- pattern: int32 [32, 2, 16], P('doc'), may hold values from 0 to 63, as said below
Outputs:
- attended: bfloat16 [32, 256, 8192], P('doc', 'ctx', 'head')
- gram: float32 [8192, 8192], P(('head', 'ctx'), 'doc')
Inputs may be any that keep to these rules, and one draw needn't show every extreme that they name: Each row pattern[d, b, :] lists 16 different block numbers; no context shard (blocks s * 32 to (s + 1) * 32 - 1) holds more than 12 of one row's blocks, and in every draw some row has exactly 12 of its blocks in one shard.
All inputs are finite; a program needn't handle non-finite values.
Results may differ from a plain program's by a relative error of at most 0.015.
Values may be sent and summed in bfloat16 or wider, within the bound.
No kernel may reach another device: no remote copies, remote signals or barrier semaphores. Data moves between devices by JAX's collectives and lax.ppermute only.
A program may use at most 128 MiB of HBM per device.

v0:
```python
import math

import jax
import jax.numpy as jnp
from jax import lax
from jax.experimental import pallas as pl
from jax.experimental.pallas import tpu as pltpu
from jax.sharding import PartitionSpec as P

HEAD_SIZE = 128
BLOCK_TOKENS = 128
NKB_DEV = 32
GROUP = 8
CAP = 12
PICKS = 16
QB = 2
NX = 4
NY = 4
NZ = 8
SLOTS = QB * CAP
SENT = 2 * SLOTS + GROUP
SCALE = HEAD_SIZE**-0.5 * math.log2(math.e)
BF16 = jnp.bfloat16
F32 = jnp.float32
ANY = pl.BlockSpec(memory_space=pl.ANY)


def hop(value, step):
    pairs = [(z * NY + y, z * NY + (y + step) % NY) for z in range(NZ) for y in range(NY)]
    return lax.ppermute(value, "doc", pairs)


def toward(value, axis):
    pairs = []
    if axis == "x":
        for c, step in ((0, 1), (1, -1)):
            pairs += [(c * NX + x, c * NX + (x + step) % NX) for x in range(NX)]
        return lax.ppermute(value, ("ctx", "head"), pairs)
    for c, step in ((0, 1), (1, -1)):
        for z in range(NZ):
            for y in range(NY):
                to_z = (z + step) % NZ if axis == "z" else z
                to_y = (y + step) % NY if axis == "y" else y
                pairs.append(((c * NZ + z) * NY + y, (c * NZ + to_z) * NY + to_y))
    return lax.ppermute(value, ("ctx", "doc"), pairs)


def swap(value):
    return lax.ppermute(value, "ctx", [(0, 1), (1, 0)])


def pack_kernel(pattern, q, k, v, sent, sem):
    c = lax.axis_index("ctx")
    other = pl.multiple_of((1 - c) * HEAD_SIZE, HEAD_SIZE)

    def copies(act):
        for g in range(GROUP):
            at = pl.multiple_of((1 - c) * GROUP * HEAD_SIZE + g * HEAD_SIZE, HEAD_SIZE)
            act(pltpu.make_async_copy(q.at[:, pl.ds(at, HEAD_SIZE)], sent.at[2 * SLOTS + g], sem))
        for b in range(QB):
            count = 0
            for s in range(PICKS):
                block = pattern[b, s]
                mine = block // NKB_DEV == c
                row = pl.multiple_of((block % NKB_DEV) * BLOCK_TOKENS, BLOCK_TOKENS)
                slot = b * CAP + count

                @pl.when(mine)
                def _(row=row, slot=slot):
                    rows = pl.ds(row, BLOCK_TOKENS)
                    cols = pl.ds(other, HEAD_SIZE)
                    act(pltpu.make_async_copy(k.at[rows, cols], sent.at[slot], sem))
                    act(pltpu.make_async_copy(v.at[rows, cols], sent.at[SLOTS + slot], sem))

                count = count + mine.astype(jnp.int32)

    copies(lambda copy: copy.start())
    copies(lambda copy: copy.wait())


def pack(pattern, q, k, v):
    return pl.pallas_call(
        pack_kernel,
        out_shape=jax.ShapeDtypeStruct((SENT, BLOCK_TOKENS, HEAD_SIZE), BF16),
        in_specs=[pl.BlockSpec(memory_space=pltpu.SMEM), ANY, ANY, ANY],
        out_specs=pl.BlockSpec(memory_space=pltpu.VMEM),
        scratch_shapes=[pltpu.SemaphoreType.DMA],
        name="pack",
    )(pattern, q, k, v)


def attend_kernel(pattern, q, k, v, got, out, turned, qs, ks, vs, sems):
    c = lax.axis_index("ctx")
    mine_cols = pl.ds(pl.multiple_of(c * HEAD_SIZE, HEAD_SIZE), HEAD_SIZE)
    for b in range(QB):

        @pl.when(c == b)
        def _(b=b):
            for g in range(GROUP):
                at = pl.multiple_of(c * GROUP * HEAD_SIZE + g * HEAD_SIZE, HEAD_SIZE)
                pltpu.make_async_copy(q.at[:, pl.ds(at, HEAD_SIZE)], qs.at[b, g], sems.at[b, 0]).start()

        @pl.when(c != b)
        def _(b=b):
            pltpu.make_async_copy(got.at[pl.ds(2 * SLOTS, GROUP)], qs.at[b], sems.at[b, 0]).start()

        for kind, (cache, chosen) in enumerate(((k, ks), (v, vs))):
            count = 0
            for s in range(PICKS):
                block = pattern[b, s]
                mine = block // NKB_DEV == c
                row = pl.multiple_of((block % NKB_DEV) * BLOCK_TOKENS, BLOCK_TOKENS)
                slot = kind * SLOTS + b * CAP + count
                sem = sems.at[b, 1 + kind]

                @pl.when(mine)
                def _(row=row, s=s, cache=cache, chosen=chosen, sem=sem, b=b):
                    src = cache.at[pl.ds(row, BLOCK_TOKENS), mine_cols]
                    pltpu.make_async_copy(src, chosen.at[b, s], sem).start()

                @pl.when(jnp.logical_not(mine))
                def _(slot=slot, s=s, chosen=chosen, sem=sem, b=b):
                    pltpu.make_async_copy(got.at[slot], chosen.at[b, s], sem).start()

                count = count + 1 - mine.astype(jnp.int32)

    for b in range(QB):
        for i, chosen in enumerate((qs, ks, vs)):
            pltpu.make_async_copy(chosen.at[b], chosen.at[b], sems.at[b, i]).wait()
        keys = ks[b].reshape(PICKS * BLOCK_TOKENS, HEAD_SIZE)
        vals = vs[b].reshape(PICKS * BLOCK_TOKENS, HEAD_SIZE)
        for pair in range(GROUP // 2):
            rows = qs[b, 2 * pair : 2 * pair + 2].reshape(2 * BLOCK_TOKENS, HEAD_SIZE)
            scores = lax.dot_general(rows, keys, (((1,), (1,)), ((), ())), preferred_element_type=F32)
            top = jnp.max(scores, axis=-1, keepdims=True)
            weights = jnp.exp2((scores - top) * SCALE)
            total = jnp.sum(weights, axis=-1, keepdims=True)
            mixed = jnp.dot(weights.astype(BF16), vals, preferred_element_type=F32) / total
            for i in range(2):
                g = 2 * pair + i
                part = mixed[i * BLOCK_TOKENS : (i + 1) * BLOCK_TOKENS]
                cols = pl.ds(g * HEAD_SIZE, HEAD_SIZE)
                out[jnp.where(c == b, 0, 1), :, cols] = part.astype(BF16)
                turned[cols, pl.ds(b * BLOCK_TOKENS, BLOCK_TOKENS)] = part.T.astype(BF16)


def attend(pattern, q, k, v, got):
    width = GROUP * HEAD_SIZE
    out = jax.ShapeDtypeStruct((QB, BLOCK_TOKENS, width), BF16)
    chosen = pltpu.VMEM((QB, PICKS, BLOCK_TOKENS, HEAD_SIZE), BF16)
    vmem = pl.BlockSpec(memory_space=pltpu.VMEM)
    return pl.pallas_call(
        attend_kernel,
        out_shape=(out, jax.ShapeDtypeStruct((width, QB * BLOCK_TOKENS), BF16)),
        in_specs=[pl.BlockSpec(memory_space=pltpu.SMEM), ANY, ANY, ANY, ANY],
        out_specs=(vmem, vmem),
        scratch_shapes=[
            pltpu.VMEM((QB, GROUP, BLOCK_TOKENS, HEAD_SIZE), BF16),
            chosen,
            chosen,
            pltpu.SemaphoreType.DMA((QB, 3)),
        ],
        compiler_params=pltpu.CompilerParams(vmem_limit_bytes=32 << 20),
        name="attend",
    )(pattern, q, k, v, got)


def right_part(refs, case, r):
    near, x1, x1_other, x2, x2_other = refs
    if case == 0:
        return near[r]
    if case == 1:
        return x1[r]
    if case == 2:
        return x1_other[1 - r]
    return (x2, x2_other)[r][...]


def product_kernel(tasks, *refs):
    both, y1, y1_other, y2, y2_other = refs[:5]
    rights, outs, bt = refs[5:10], refs[10:-1], refs[-1]
    c, x = lax.axis_index("ctx"), lax.axis_index("head")
    z = lax.axis_index("doc") // NY
    for i in sorted({i for i, _ in tasks}):
        owner = lax.rem(z + jnp.where(c == 0, 4 - i, 4 + i), NZ)
        away = lax.rem(owner // 2 + NX - x, NX)
        other = (lax.rem(owner, 2) != c).astype(jnp.int32)
        side = jnp.where(c == 0, 3, 1)
        case = jnp.where(away == 0, 0, jnp.where(away == 2, 3, jnp.where(away == side, 1, 2)))
        for k in range(4):
            for r in range(2):

                @pl.when(jnp.logical_and(case == k, other == r))
                def _(k=k, r=r):
                    bt[...] = right_part(rights, k, r)

        for r in sorted({r for j, r in tasks if j == i}):
            total = None
            lefts = (both[r], y1[r], y1_other[1 - r], (y2, y2_other)[r][...])
            for left, doc in zip(lefts, (0, 1 + c, 2 - c, 3)):
                dims = (((1,), (1,)), ((), ()))
                term = lax.dot_general(left, bt[doc], dims, preferred_element_type=F32)
                total = term if total is None else total + term
            out = outs[tasks.index((i, r))]
            out[...] = total.astype(out.dtype)


def products(tasks, lefts, rights):
    rows, cols = GROUP * HEAD_SIZE, 2 * HEAD_SIZE
    vmem = pl.BlockSpec(memory_space=pltpu.VMEM)

    def body(*refs):
        product_kernel(tasks, *refs)

    return pl.pallas_call(
        body,
        out_shape=[jax.ShapeDtypeStruct((rows, cols), F32 if i == 4 else BF16) for i, _ in tasks],
        in_specs=[vmem] * 10,
        out_specs=[vmem] * len(tasks),
        scratch_shapes=[pltpu.VMEM((NY, cols, QB * BLOCK_TOKENS), BF16)],
        compiler_params=pltpu.CompilerParams(vmem_limit_bytes=16 << 20),
        name="products",
    )(*lefts, *rights)


def added(got, here):
    return (got.astype(F32) + here.astype(F32)).astype(BF16)


def per_device(queries, keys, values, pattern):
    c = lax.axis_index("ctx")
    y = lax.axis_index("doc") % NY
    q, k, v, chosen = queries[0], keys[0], values[0], pattern[0]
    got = swap(pack(chosen, q, k, v))
    out, turned = attend(chosen, q, k, v, got)
    cols = 2 * HEAD_SIZE

    def share(step):
        return lax.dynamic_slice_in_dim(turned, ((y + step) % NY) * cols, cols, 0)

    mine = jnp.stack([share(0), hop(share(1), 1), hop(share(-1), -1), hop(share(2), 2)])
    both = jnp.stack([turned, swap(turned)])
    near = jnp.stack([mine, swap(mine)])
    y1 = toward(both, "y")
    x1 = toward(near, "x")
    x2 = toward(x1[0], "x")
    y2 = toward(y1[0], "y")
    lefts = [both, y1, swap(y1), y2, swap(y2)]
    rights = [near, x1, swap(x1), x2, swap(x2)]

    [first] = products([(0, 0)], lefts, rights)
    second = products([(1, 0), (1, 1)], lefts, rights)
    third = products([(2, 0), (2, 1), (3, 0), (3, 1), (4, 0)], lefts, rights)
    long = toward(first, "z")
    short = toward(second[1], "z")
    long = toward(added(long, second[0]), "z")
    short = toward(added(short, third[1]), "z")
    long = toward(added(long, third[0]), "z")
    short = toward(added(short, third[3]), "z")
    long = toward(added(long, third[2]), "z")
    gram = third[4] + swap(short).astype(F32) + long.astype(F32)

    own, returned = out[0], swap(out[1])
    attended = jnp.where(
        c == 0,
        jnp.concatenate([own, returned], axis=1),
        jnp.concatenate([returned, own], axis=1),
    )
    return (attended[None], gram)


def solution(mesh):
    placed = (
        P("doc", "ctx", "head"),
        P("doc", "ctx", "head"),
        P("doc", "ctx", "head"),
        P("doc", None, None),
    )
    return jax.shard_map(
        per_device,
        mesh=mesh,
        in_specs=placed,
        out_specs=(P("doc", "ctx", "head"), P(("head", "ctx"), "doc")),
        check_vma=False,
    )
```

profile of v0, /device:TPU:8, one launch (start us, length us, event | category | flops | bytes accessed | tf_op | source)
XLA Modules:
  0.0 108.2 jit_solution(1979867285691444863)
XLA Ops:
  0.7 3.3 %pack.1 = bf16[56,128,128]{2,1,0:T(8,128)(2,1)} custom-call(s32[2,16]{1,0:T(2,128)} %bitcast.28, bf16[128,2048]{1,0:T(8,128)(2,1)} %bitcast.26, bf16[4096,256]{1,0:T(8,128)(2,1)} %bitcast.21, bf16[4096,256]{1,0:T(8,128)(2,1)} %bitcast.23), custom_call_target="tpu_custom_call" | custom-call | tf_op jit(solution)/shard_map/pack/pallas_call | solution.py:82
  4.2 4.0 %collective-permute-done.got = bf16[56,128,128]{2,1,0:T(8,128)(2,1)} collective-permute-done((bf16[56,128,128]{2,1,0:T(8,128)(2,1)}, bf16[56,128,128]{2,1,0:T(8,128)(2,1)}, u32[]{:S(2)}, u32[]{:S(2)}) %collective-permute-start) | collective-permute-done | bytes 1835040 | tf_op jit(solution)/shard_map/ppermute | solution.py:49
  8.2 1.6 %copy-done.1 = bf16[1,4096,256]{2,1,0:T(8,128)(2,1)S(1)} copy-done((bf16[1,4096,256]{2,1,0:T(8,128)(2,1)S(1)}, bf16[1,4096,256]{2,1,0:T(8,128)(2,1)}, u32[]{:S(2)}) %copy-start.1) | copy-done | bytes 2097176
  9.8 8.8 %attend.1 = (bf16[2,128,1024]{2,1,0:T(8,128)(2,1)S(1)}, bf16[1024,256]{1,0:T(8,128)(2,1)S(1)}) custom-call(s32[2,16]{1,0:T(2,128)S(1)} %bitcast.29, bf16[128,2048]{1,0:T(8,128)(2,1)S(1)} %bitcast.27, bf16[4096,256]{1,0:T(8,128)(2,1)S(1)} %bitcast.22, bf16[4096,256]{1,0:T(8,128)(2,1)S(1)} %bitcast.24, bf16[56,128,128]{2,1,0:T(8,128)(2,1)} %collective-permute-done.got), custom_call_target="tpu_custom_call" | custom-call | tf_op jit(solution)/shard_map/attend/pallas_call | solution.py:152
  18.7 2.5 %collective-permute-start.9 = (bf16[256,256]{1,0:T(8,128)(2,1)S(1)}, bf16[256,256]{1,0:T(8,128)(2,1)S(1)}, u32[]{:S(2)}, u32[]{:S(2)}) collective-permute-start(bf16[256,256]{1,0:T(8,128)(2,1)S(1)} %get-tuple-element.23), channel_id=1, source_target_pairs={{0,2},{1,3},{2,0},{3,1},{4,6},{5,7},{6,4},{7,5},{8,10},{9,11},{10,... | collective-permute-start | bytes 393224 | tf_op jit(solution)/shard_map/ppermute | solution.py:30
  21.1 1.4 %collective-permute-start.8 = (bf16[256,256]{1,0:T(8,128)(2,1)S(1)}, bf16[256,256]{1,0:T(8,128)(2,1)S(1)}, u32[]{:S(2)}, u32[]{:S(2)}) collective-permute-start(bf16[256,256]{1,0:T(8,128)(2,1)S(1)} %get-tuple-element.24), channel_id=1, source_target_pairs={{0,3},{1,0},{2,1},{3,2},{4,7},{5,4},{6,5},{7,6},{8,11},{9,8},{10,9... | collective-permute-start | bytes 393224 | tf_op jit(solution)/shard_map/ppermute | solution.py:30
  22.5 0.6 collective-permute-start.7
  23.2 3.4 %collective-permute-done.9 = bf16[256,256]{1,0:T(8,128)(2,1)S(1)} collective-permute-done((bf16[256,256]{1,0:T(8,128)(2,1)S(1)}, bf16[256,256]{1,0:T(8,128)(2,1)S(1)}, u32[]{:S(2)}, u32[]{:S(2)}) %collective-permute-start.9) | collective-permute-done | bytes 131104 | tf_op jit(solution)/shard_map/ppermute | solution.py:30
  26.6 2.0 %collective-permute-done.8 = bf16[256,256]{1,0:T(8,128)(2,1)S(1)} collective-permute-done((bf16[256,256]{1,0:T(8,128)(2,1)S(1)}, bf16[256,256]{1,0:T(8,128)(2,1)S(1)}, u32[]{:S(2)}, u32[]{:S(2)}) %collective-permute-start.8) | collective-permute-done | bytes 131104 | tf_op jit(solution)/shard_map/ppermute | solution.py:30
  29.1 1.5 %collective-permute-start.3 = (bf16[2,1024,256]{2,1,0:T(8,128)(2,1)S(1)}, bf16[2,1024,256]{2,1,0:T(8,128)(2,1)S(1)}, u32[]{:S(2)}, u32[]{:S(2)}) collective-permute-start(bf16[2,1024,256]{2,1,0:T(8,128)(2,1)S(1)} %pad_maximum_fusion.refs_0_), channel_id=1, source_target_pairs={{0,1},{1,2},{2,3},{3,0},{4,5},{5,6},{6,7},{7,4},{8,9},{9,10},{10,1... | collective-permute-start | bytes 3145736 | tf_op jit(solution)/shard_map/ppermute | solution.py:45
  30.9 1.6 %collective-permute-start.11 = (bf16[2,4,256,256]{3,2,1,0:T(8,128)(2,1)S(1)}, bf16[2,4,256,256]{3,2,1,0:T(8,128)(2,1)S(1)}, u32[]{:S(2)}, u32[]{:S(2)}) collective-permute-start(bf16[2,4,256,256]{3,2,1,0:T(8,128)(2,1)S(1)} %pad_maximum_fusion.1.refs_5_), channel_id=1, source_target_pairs={{0,32},{32,64},{64,96},{96,0},{128,224},{160,128},{192,160},{224,1... | collective-permute-start | bytes 3145736 | tf_op jit(solution)/shard_map/ppermute | solution.py:38
  32.5 11.5 %collective-permute-done.3.refs_1_ = bf16[2,1024,256]{2,1,0:T(8,128)(2,1)S(1)} collective-permute-done((bf16[2,1024,256]{2,1,0:T(8,128)(2,1)S(1)}, bf16[2,1024,256]{2,1,0:T(8,128)(2,1)S(1)}, u32[]{:S(2)}, u32[]{:S(2)}) %collective-permute-start.3) | collective-permute-done | bytes 1048608 | tf_op jit(solution)/shard_map/ppermute | solution.py:45
  44.1 1.4 %collective-permute-start.5 = (bf16[1024,256]{1,0:T(8,128)(2,1)S(1)}, bf16[1024,256]{1,0:T(8,128)(2,1)S(1)}, u32[]{:S(2)}, u32[]{:S(2)}) collective-permute-start(bf16[1024,256]{1,0:T(8,128)(2,1)S(1)} %slice_bitcast_fusion.1), channel_id=1, source_target_pairs={{0,1},{1,2},{2,3},{3,0},{4,5},{5,6},{6,7},{7,4},{8,9},{9,10},{10,1... | collective-permute-start | bytes 1572872 | tf_op jit(solution)/shard_map/ppermute | solution.py:45
  45.5 1.5 %collective-permute-done.11.refs_6_ = bf16[2,4,256,256]{3,2,1,0:T(8,128)(2,1)S(1)} collective-permute-done((bf16[2,4,256,256]{3,2,1,0:T(8,128)(2,1)S(1)}, bf16[2,4,256,256]{3,2,1,0:T(8,128)(2,1)S(1)}, u32[]{:S(2)}, u32[]{:S(2)}) %collective-permute-start.11) | collective-permute-done | bytes 1048608 | tf_op jit(solution)/shard_map/ppermute | solution.py:38
  47.4 1.2 %collective-permute-start.12 = (bf16[2,4,256,256]{3,2,1,0:T(8,128)(2,1)S(1)}, bf16[2,4,256,256]{3,2,1,0:T(8,128)(2,1)S(1)}, u32[]{:S(2)}, u32[]{:S(2)}) collective-permute-start(bf16[2,4,256,256]{3,2,1,0:T(8,128)(2,1)S(1)} %collective-permute-done.11.refs_6_), channel_id=1, source_target_pairs={{0,128},{128,0},{1,129},{129,1},{2,130},{130,2},{3,131},{131,3},{4... | collective-permute-start | bytes 3145736 | tf_op jit(solution)/shard_map/ppermute | solution.py:49
  48.6 5.9 %collective-permute-done.5.refs_3_ = bf16[1024,256]{1,0:T(8,128)(2,1)S(1)} collective-permute-done((bf16[1024,256]{1,0:T(8,128)(2,1)S(1)}, bf16[1024,256]{1,0:T(8,128)(2,1)S(1)}, u32[]{:S(2)}, u32[]{:S(2)}) %collective-permute-start.5) | collective-permute-done | bytes 524320 | tf_op jit(solution)/shard_map/ppermute | solution.py:45
  54.6 3.0 %collective-permute-done.13.refs_8_ = bf16[4,256,256]{2,1,0:T(8,128)(2,1)S(1)} collective-permute-done((bf16[4,256,256]{2,1,0:T(8,128)(2,1)S(1)}, bf16[4,256,256]{2,1,0:T(8,128)(2,1)S(1)}, u32[]{:S(2)}, u32[]{:S(2)}) %collective-permute-start.13) | collective-permute-done | bytes 524320 | tf_op jit(solution)/shard_map/ppermute | solution.py:38
  57.5 1.9 %collective-permute-done.14.refs_9_ = bf16[4,256,256]{2,1,0:T(8,128)(2,1)S(1)} collective-permute-done((bf16[4,256,256]{2,1,0:T(8,128)(2,1)S(1)}, bf16[4,256,256]{2,1,0:T(8,128)(2,1)S(1)}, u32[]{:S(2)}, u32[]{:S(2)}) %collective-permute-start.14) | collective-permute-done | bytes 524320 | tf_op jit(solution)/shard_map/ppermute | solution.py:49
  59.4 0.8 products.5
  60.2 2.0 %collective-permute-start.19 = (bf16[1024,256]{1,0:T(8,128)(2,1)S(1)}, bf16[1024,256]{1,0:T(8,128)(2,1)S(1)}, u32[]{:S(2)}, u32[]{:S(2)}) collective-permute-start(bf16[1024,256]{1,0:T(8,128)(2,1)S(1)} %products.5), channel_id=1, source_target_pairs={{0,4},{1,5},{2,6},{3,7},{4,8},{5,9},{6,10},{7,11},{8,12},{9,13},{1... | collective-permute-start | bytes 1572872 | tf_op jit(solution)/shard_map/ppermute | solution.py:45
  62.2 1.3 %products.4 = (bf16[1024,256]{1,0:T(8,128)(2,1)S(1)}, bf16[1024,256]{1,0:T(8,128)(2,1)S(1)}) custom-call(bf16[2,1024,256]{2,1,0:T(8,128)(2,1)S(1)} %pad_maximum_fusion.refs_0_, bf16[2,1024,256]{2,1,0:T(8,128)(2,1)S(1)} %collective-permute-done.3.refs_1_, bf16[2,1024,256]{2,1,0:T(8,128)(2,1)S(1)} %collective-permute-done.4.refs_2_, ...), custom_call_target="tpu_custom_call" | custom-call | tf_op jit(solution)/shard_map/products/pallas_call | solution.py:215
  63.5 2.1 %collective-permute-start.15 = (bf16[1024,256]{1,0:T(8,128)(2,1)S(1)}, bf16[1024,256]{1,0:T(8,128)(2,1)S(1)}, u32[]{:S(2)}, u32[]{:S(2)}) collective-permute-start(bf16[1024,256]{1,0:T(8,128)(2,1)S(1)} %get-tuple-element.14), channel_id=1, source_target_pairs={{0,4},{1,5},{2,6},{3,7},{4,8},{5,9},{6,10},{7,11},{8,12},{9,13},{1... | collective-permute-start | bytes 1572872 | tf_op jit(solution)/shard_map/ppermute | solution.py:45
  65.6 7.8 %collective-permute-done.19 = bf16[1024,256]{1,0:T(8,128)(2,1)S(1)} collective-permute-done((bf16[1024,256]{1,0:T(8,128)(2,1)S(1)}, bf16[1024,256]{1,0:T(8,128)(2,1)S(1)}, u32[]{:S(2)}, u32[]{:S(2)}) %collective-permute-start.19) | collective-permute-done | bytes 524320 | tf_op jit(solution)/shard_map/ppermute | solution.py:45
  73.6 4.8 %products.3 = (bf16[1024,256]{1,0:T(8,128)(2,1)S(1)}, bf16[1024,256]{1,0:T(8,128)(2,1)S(1)}, bf16[1024,256]{1,0:T(8,128)(2,1)S(1)}, bf16[1024,256]{1,0:T(8,128)(2,1)S(1)}, f32[1024,256]{1,0:T(8,128)S(1)}) custom-call(bf16[2,1024,256]{2,1,0:T(8,128)(2,1)S(1)} %pad_maximum_fusion.refs_0_, bf16[2,1024,256]{2,1,0:T(8,128)(2,1)S(1)} %collective-permute-done.3.refs_1_, ...), custom_call_target="tpu_custom_call" | custom-call | tf_op jit(solution)/shard_map/products/pallas_call | solution.py:215
  79.2 5.4 %collective-permute-done.20 = bf16[1024,256]{1,0:T(8,128)(2,1)S(1)} collective-permute-done((bf16[1024,256]{1,0:T(8,128)(2,1)S(1)}, bf16[1024,256]{1,0:T(8,128)(2,1)S(1)}, u32[]{:S(2)}, u32[]{:S(2)}) %collective-permute-start.20) | collective-permute-done | bytes 524320 | tf_op jit(solution)/shard_map/ppermute | solution.py:45
  84.8 5.4 %collective-permute-done.16 = bf16[1024,256]{1,0:T(8,128)(2,1)S(1)} collective-permute-done((bf16[1024,256]{1,0:T(8,128)(2,1)S(1)}, bf16[1024,256]{1,0:T(8,128)(2,1)S(1)}, u32[]{:S(2)}, u32[]{:S(2)}) %collective-permute-start.16) | collective-permute-done | bytes 524320 | tf_op jit(solution)/shard_map/ppermute | solution.py:45
  90.4 5.4 %collective-permute-done.21 = bf16[1024,256]{1,0:T(8,128)(2,1)S(1)} collective-permute-done((bf16[1024,256]{1,0:T(8,128)(2,1)S(1)}, bf16[1024,256]{1,0:T(8,128)(2,1)S(1)}, u32[]{:S(2)}, u32[]{:S(2)}) %collective-permute-start.21) | collective-permute-done | bytes 524320 | tf_op jit(solution)/shard_map/ppermute | solution.py:45
  96.0 5.5 %collective-permute-done.17 = bf16[1024,256]{1,0:T(8,128)(2,1)} collective-permute-done((bf16[1024,256]{1,0:T(8,128)(2,1)S(1)}, bf16[1024,256]{1,0:T(8,128)(2,1)}, u32[]{:S(2)}, u32[]{:S(2)}) %collective-permute-start.17) | collective-permute-done | bytes 524320 | tf_op jit(solution)/shard_map/ppermute | solution.py:45
  102.2 1.6 %collective-permute-done.1 = bf16[128,1024]{1,0:T(8,128)(2,1)S(1)} collective-permute-done((bf16[128,1024]{1,0:T(8,128)(2,1)S(1)}, bf16[128,1024]{1,0:T(8,128)(2,1)S(1)}, u32[]{:S(2)}, u32[]{:S(2)}) %collective-permute-start.1) | collective-permute-done | bytes 262176 | tf_op jit(solution)/shard_map/ppermute | solution.py:49
  103.8 0.9 maximum_select_fusion
  104.7 2.3 %collective-permute-done.22 = bf16[1024,256]{1,0:T(8,128)(2,1)S(1)} collective-permute-done((bf16[1024,256]{1,0:T(8,128)(2,1)S(1)}, bf16[1024,256]{1,0:T(8,128)(2,1)S(1)}, u32[]{:S(2)}, u32[]{:S(2)}) %collective-permute-start.22) | collective-permute-done | bytes 524320 | tf_op jit(solution)/shard_map/ppermute | solution.py:45
  107.0 1.1 %convert_add_fusion = f32[1024,256]{1,0:T(8,128)} fusion(bf16[1024,256]{1,0:T(8,128)(2,1)S(1)} %collective-permute-done.22, f32[1024,256]{1,0:T(8,128)S(1)} %get-tuple-element.13, bf16[1024,256]{1,0:T(8,128)(2,1)S(1)} %collective-permute-done.18), kind=kLoop, calls=%fused_computation.2 | loop fusion | flops 1048576 | bytes 3145728 | tf_op jit(solution)/shard_map/add | solution.py:261
  (41 shorter events, 3.7 us)
Async XLA Ops:
  0.6 7.6 %copy-start = (bf16[1,4096,256]{2,1,0:T(8,128)(2,1)S(1)}, bf16[1,4096,256]{2,1,0:T(8,128)(2,1)}, u32[]{:S(2)}) copy-start(bf16[1,4096,256]{2,1,0:T(8,128)(2,1)} %param.5) | copy-start | bytes 6291460
  0.6 7.6 %copy-start.2 = (bf16[1,128,2048]{2,1,0:T(8,128)(2,1)S(1)}, bf16[1,128,2048]{2,1,0:T(8,128)(2,1)}, u32[]{:S(2)}) copy-start(bf16[1,128,2048]{2,1,0:T(8,128)(2,1)} %param.4) | copy-start | bytes 1572868
  0.6 7.6 %copy-start.3 = (s32[1,2,16]{2,1,0:T(2,128)S(1)}, s32[1,2,16]{2,1,0:T(2,128)}, u32[]{:S(2)}) copy-start(s32[1,2,16]{2,1,0:T(2,128)} %param.7) | copy-start | bytes 388
  4.0 4.2 %collective-permute-start = (bf16[56,128,128]{2,1,0:T(8,128)(2,1)}, bf16[56,128,128]{2,1,0:T(8,128)(2,1)}, u32[]{:S(2)}, u32[]{:S(2)}) collective-permute-start(bf16[56,128,128]{2,1,0:T(8,128)(2,1)} %pack.1), channel_id=1, source_target_pairs={{0,128},{128,0},{1,129},{129,1},{2,130},{130,2},{3,131},{131,3},{4... | collective-permute-start | bytes 5505032 | tf_op jit(solution)/shard_map/ppermute | solution.py:49
  8.2 1.6 %copy-start.1 = (bf16[1,4096,256]{2,1,0:T(8,128)(2,1)S(1)}, bf16[1,4096,256]{2,1,0:T(8,128)(2,1)}, u32[]{:S(2)}) copy-start(bf16[1,4096,256]{2,1,0:T(8,128)(2,1)} %param.6) | copy-start | bytes 6291460
  18.7 7.9 %collective-permute-start.9 = (bf16[256,256]{1,0:T(8,128)(2,1)S(1)}, bf16[256,256]{1,0:T(8,128)(2,1)S(1)}, u32[]{:S(2)}, u32[]{:S(2)}) collective-permute-start(bf16[256,256]{1,0:T(8,128)(2,1)S(1)} %get-tuple-element.23), channel_id=1, source_target_pairs={{0,2},{1,3},{2,0},{3,1},{4,6},{5,7},{6,4},{7,5},{8,10},{9,11},{10,... | collective-permute-start | bytes 393224 | tf_op jit(solution)/shard_map/ppermute | solution.py:30
  21.1 7.4 %collective-permute-start.8 = (bf16[256,256]{1,0:T(8,128)(2,1)S(1)}, bf16[256,256]{1,0:T(8,128)(2,1)S(1)}, u32[]{:S(2)}, u32[]{:S(2)}) collective-permute-start(bf16[256,256]{1,0:T(8,128)(2,1)S(1)} %get-tuple-element.24), channel_id=1, source_target_pairs={{0,3},{1,0},{2,1},{3,2},{4,7},{5,4},{6,5},{7,6},{8,11},{9,8},{10,9... | collective-permute-start | bytes 393224 | tf_op jit(solution)/shard_map/ppermute | solution.py:30
  22.5 6.2 %collective-permute-start.7 = (bf16[256,256]{1,0:T(8,128)(2,1)S(1)}, bf16[256,256]{1,0:T(8,128)(2,1)S(1)}, u32[]{:S(2)}, u32[]{:S(2)}) collective-permute-start(bf16[256,256]{1,0:T(8,128)(2,1)S(1)} %get-tuple-element.25), channel_id=1, source_target_pairs={{0,1},{1,2},{2,3},{3,0},{4,5},{5,6},{6,7},{7,4},{8,9},{9,10},{10,1... | collective-permute-start | bytes 393224 | tf_op jit(solution)/shard_map/ppermute | solution.py:30
  23.2 5.8 %collective-permute-start.2 = (bf16[1024,256]{1,0:T(8,128)(2,1)S(1)}, bf16[1024,256]{1,0:T(8,128)(2,1)S(1)}, u32[]{:S(2)}, u32[]{:S(2)}) collective-permute-start(bf16[1024,256]{1,0:T(8,128)(2,1)S(1)} %get-tuple-element.12), channel_id=1, source_target_pairs={{0,128},{128,0},{1,129},{129,1},{2,130},{130,2},{3,131},{131,3},{4... | collective-permute-start | bytes 1572872 | tf_op jit(solution)/shard_map/ppermute | solution.py:49
  28.8 2.0 %collective-permute-start.10 = (bf16[4,256,256]{2,1,0:T(8,128)(2,1)S(1)}, bf16[4,256,256]{2,1,0:T(8,128)(2,1)S(1)}, u32[]{:S(2)}, u32[]{:S(2)}) collective-permute-start(bf16[4,256,256]{2,1,0:T(8,128)(2,1)S(1)} %get-tuple-element.21), channel_id=1, source_target_pairs={{0,128},{128,0},{1,129},{129,1},{2,130},{130,2},{3,131},{131,3},{4... | collective-permute-start | bytes 1572872 | tf_op jit(solution)/shard_map/ppermute | solution.py:49
  29.1 15.0 %collective-permute-start.3 = (bf16[2,1024,256]{2,1,0:T(8,128)(2,1)S(1)}, bf16[2,1024,256]{2,1,0:T(8,128)(2,1)S(1)}, u32[]{:S(2)}, u32[]{:S(2)}) collective-permute-start(bf16[2,1024,256]{2,1,0:T(8,128)(2,1)S(1)} %pad_maximum_fusion.refs_0_), channel_id=1, source_target_pairs={{0,1},{1,2},{2,3},{3,0},{4,5},{5,6},{6,7},{7,4},{8,9},{9,10},{10,1... | collective-permute-start | bytes 3145736 | tf_op jit(solution)/shard_map/ppermute | solution.py:45
  30.9 16.1 %collective-permute-start.11 = (bf16[2,4,256,256]{3,2,1,0:T(8,128)(2,1)S(1)}, bf16[2,4,256,256]{3,2,1,0:T(8,128)(2,1)S(1)}, u32[]{:S(2)}, u32[]{:S(2)}) collective-permute-start(bf16[2,4,256,256]{3,2,1,0:T(8,128)(2,1)S(1)} %pad_maximum_fusion.1.refs_5_), channel_id=1, source_target_pairs={{0,32},{32,64},{64,96},{96,0},{128,224},{160,128},{192,160},{224,1... | collective-permute-start | bytes 3145736 | tf_op jit(solution)/shard_map/ppermute | solution.py:38
  44.1 10.5 %collective-permute-start.5 = (bf16[1024,256]{1,0:T(8,128)(2,1)S(1)}, bf16[1024,256]{1,0:T(8,128)(2,1)S(1)}, u32[]{:S(2)}, u32[]{:S(2)}) collective-permute-start(bf16[1024,256]{1,0:T(8,128)(2,1)S(1)} %slice_bitcast_fusion.1), channel_id=1, source_target_pairs={{0,1},{1,2},{2,3},{3,0},{4,5},{5,6},{6,7},{7,4},{8,9},{9,10},{10,1... | collective-permute-start | bytes 1572872 | tf_op jit(solution)/shard_map/ppermute | solution.py:45
  45.5 12.0 %collective-permute-start.4 = (bf16[2,1024,256]{2,1,0:T(8,128)(2,1)S(1)}, bf16[2,1024,256]{2,1,0:T(8,128)(2,1)S(1)}, u32[]{:S(2)}, u32[]{:S(2)}) collective-permute-start(bf16[2,1024,256]{2,1,0:T(8,128)(2,1)S(1)} %collective-permute-done.3.refs_1_), channel_id=1, source_target_pairs={{0,128},{128,0},{1,129},{129,1},{2,130},{130,2},{3,131},{131,3},{4... | collective-permute-start | bytes 3145736 | tf_op jit(solution)/shard_map/ppermute | solution.py:49
  47.1 10.5 %collective-permute-start.13 = (bf16[4,256,256]{2,1,0:T(8,128)(2,1)S(1)}, bf16[4,256,256]{2,1,0:T(8,128)(2,1)S(1)}, u32[]{:S(2)}, u32[]{:S(2)}) collective-permute-start(bf16[4,256,256]{2,1,0:T(8,128)(2,1)S(1)} %slice_bitcast_fusion), channel_id=1, source_target_pairs={{0,32},{32,64},{64,96},{96,0},{128,224},{160,128},{192,160},{224,1... | collective-permute-start | bytes 1572872 | tf_op jit(solution)/shard_map/ppermute | solution.py:38
  47.4 12.0 %collective-permute-start.12 = (bf16[2,4,256,256]{3,2,1,0:T(8,128)(2,1)S(1)}, bf16[2,4,256,256]{3,2,1,0:T(8,128)(2,1)S(1)}, u32[]{:S(2)}, u32[]{:S(2)}) collective-permute-start(bf16[2,4,256,256]{3,2,1,0:T(8,128)(2,1)S(1)} %collective-permute-done.11.refs_6_), channel_id=1, source_target_pairs={{0,128},{128,0},{1,129},{129,1},{2,130},{130,2},{3,131},{131,3},{4... | collective-permute-start | bytes 3145736 | tf_op jit(solution)/shard_map/ppermute | solution.py:49
  54.6 3.0 %collective-permute-start.6 = (bf16[1024,256]{1,0:T(8,128)(2,1)S(1)}, bf16[1024,256]{1,0:T(8,128)(2,1)S(1)}, u32[]{:S(2)}, u32[]{:S(2)}) collective-permute-start(bf16[1024,256]{1,0:T(8,128)(2,1)S(1)} %collective-permute-done.5.refs_3_), channel_id=1, source_target_pairs={{0,128},{128,0},{1,129},{129,1},{2,130},{130,2},{3,131},{131,3},{4... | collective-permute-start | bytes 1572872 | tf_op jit(solution)/shard_map/ppermute | solution.py:49
  57.5 1.9 %collective-permute-start.14 = (bf16[4,256,256]{2,1,0:T(8,128)(2,1)S(1)}, bf16[4,256,256]{2,1,0:T(8,128)(2,1)S(1)}, u32[]{:S(2)}, u32[]{:S(2)}) collective-permute-start(bf16[4,256,256]{2,1,0:T(8,128)(2,1)S(1)} %collective-permute-done.13.refs_8_), channel_id=1, source_target_pairs={{0,128},{128,0},{1,129},{129,1},{2,130},{130,2},{3,131},{131,3},{4... | collective-permute-start | bytes 1572872 | tf_op jit(solution)/shard_map/ppermute | solution.py:49
  60.2 13.1 %collective-permute-start.19 = (bf16[1024,256]{1,0:T(8,128)(2,1)S(1)}, bf16[1024,256]{1,0:T(8,128)(2,1)S(1)}, u32[]{:S(2)}, u32[]{:S(2)}) collective-permute-start(bf16[1024,256]{1,0:T(8,128)(2,1)S(1)} %products.5), channel_id=1, source_target_pairs={{0,4},{1,5},{2,6},{3,7},{4,8},{5,9},{6,10},{7,11},{8,12},{9,13},{1... | collective-permute-start | bytes 1572872 | tf_op jit(solution)/shard_map/ppermute | solution.py:45
  63.5 15.4 %collective-permute-start.15 = (bf16[1024,256]{1,0:T(8,128)(2,1)S(1)}, bf16[1024,256]{1,0:T(8,128)(2,1)S(1)}, u32[]{:S(2)}, u32[]{:S(2)}) collective-permute-start(bf16[1024,256]{1,0:T(8,128)(2,1)S(1)} %get-tuple-element.14), channel_id=1, source_target_pairs={{0,4},{1,5},{2,6},{3,7},{4,8},{5,9},{6,10},{7,11},{8,12},{9,13},{1... | collective-permute-start | bytes 1572872 | tf_op jit(solution)/shard_map/ppermute | solution.py:45
  73.5 11.1 %collective-permute-start.20 = (bf16[1024,256]{1,0:T(8,128)(2,1)S(1)}, bf16[1024,256]{1,0:T(8,128)(2,1)S(1)}, u32[]{:S(2)}, u32[]{:S(2)}) collective-permute-start(bf16[1024,256]{1,0:T(8,128)(2,1)S(1)} %add_convert_fusion.2), channel_id=1, source_target_pairs={{0,4},{1,5},{2,6},{3,7},{4,8},{5,9},{6,10},{7,11},{8,12},{9,13},{1... | collective-permute-start | bytes 1572872 | tf_op jit(solution)/shard_map/ppermute | solution.py:45
  79.1 11.1 %collective-permute-start.16 = (bf16[1024,256]{1,0:T(8,128)(2,1)S(1)}, bf16[1024,256]{1,0:T(8,128)(2,1)S(1)}, u32[]{:S(2)}, u32[]{:S(2)}) collective-permute-start(bf16[1024,256]{1,0:T(8,128)(2,1)S(1)} %add_convert_fusion.4), channel_id=1, source_target_pairs={{0,4},{1,5},{2,6},{3,7},{4,8},{5,9},{6,10},{7,11},{8,12},{9,13},{1... | collective-permute-start | bytes 1572872 | tf_op jit(solution)/shard_map/ppermute | solution.py:45
  84.7 11.1 %collective-permute-start.21 = (bf16[1024,256]{1,0:T(8,128)(2,1)S(1)}, bf16[1024,256]{1,0:T(8,128)(2,1)S(1)}, u32[]{:S(2)}, u32[]{:S(2)}) collective-permute-start(bf16[1024,256]{1,0:T(8,128)(2,1)S(1)} %add_convert_fusion.1), channel_id=1, source_target_pairs={{0,4},{1,5},{2,6},{3,7},{4,8},{5,9},{6,10},{7,11},{8,12},{9,13},{1... | collective-permute-start | bytes 1572872 | tf_op jit(solution)/shard_map/ppermute | solution.py:45
  90.3 11.2 %collective-permute-start.17 = (bf16[1024,256]{1,0:T(8,128)(2,1)S(1)}, bf16[1024,256]{1,0:T(8,128)(2,1)}, u32[]{:S(2)}, u32[]{:S(2)}) collective-permute-start(bf16[1024,256]{1,0:T(8,128)(2,1)S(1)} %add_convert_fusion.3), channel_id=1, source_target_pairs={{0,4},{1,5},{2,6},{3,7},{4,8},{5,9},{6,10},{7,11},{8,12},{9,13},{1... | collective-permute-start | bytes 1572872 | tf_op jit(solution)/shard_map/ppermute | solution.py:45
  95.9 11.1 %collective-permute-start.22 = (bf16[1024,256]{1,0:T(8,128)(2,1)S(1)}, bf16[1024,256]{1,0:T(8,128)(2,1)S(1)}, u32[]{:S(2)}, u32[]{:S(2)}) collective-permute-start(bf16[1024,256]{1,0:T(8,128)(2,1)S(1)} %add_convert_fusion), channel_id=1, source_target_pairs={{0,4},{1,5},{2,6},{3,7},{4,8},{5,9},{6,10},{7,11},{8,12},{9,13},{1... | collective-permute-start | bytes 1572872 | tf_op jit(solution)/shard_map/ppermute | solution.py:45
  101.5 5.5 %collective-permute-start.18 = (bf16[1024,256]{1,0:T(8,128)(2,1)}, bf16[1024,256]{1,0:T(8,128)(2,1)S(1)}, u32[]{:S(2)}, u32[]{:S(2)}) collective-permute-start(bf16[1024,256]{1,0:T(8,128)(2,1)} %collective-permute-done.17), channel_id=1, source_target_pairs={{0,128},{128,0},{1,129},{129,1},{2,130},{130,2},{3,131},{131,3},{4... | collective-permute-start | bytes 1572872 | tf_op jit(solution)/shard_map/ppermute | solution.py:49
  101.6 2.2 %collective-permute-start.1 = (bf16[128,1024]{1,0:T(8,128)(2,1)S(1)}, bf16[128,1024]{1,0:T(8,128)(2,1)S(1)}, u32[]{:S(2)}, u32[]{:S(2)}) collective-permute-start(bf16[128,1024]{1,0:T(8,128)(2,1)S(1)} %get-tuple-element.27), channel_id=1, source_target_pairs={{0,128},{128,0},{1,129},{129,1},{2,130},{130,2},{3,131},{131,3},{4... | collective-permute-start | bytes 786440 | tf_op jit(solution)/shard_map/ppermute | solution.py:49
where the time goes:
time: 109 us; the launch traced here: 108 us
  waiting for transfers between devices  67.7 us (62%)
  Pallas kernels  19 us (17%)
  starting transfers between devices  15.8 us (14%)
  other arithmetic  2.96 us (3%)
  local copies, waits for them, and re-layouts  1.75 us (2%)
    ppermute x9, waiting for transfers between devices, toward(): return lax.ppermute(value, ('ctx', 'doc'), pairs)  49.8 us
    pallas_call x1, Pallas kernels, attend(): pl.pallas_call(attend_kernel, out_shape=(out, jax.ShapeDtypeStruct((width...  8.77 us
    ppermute x9, waiting for transfers between devices, swap(): return lax.ppermute(value, 'ctx', [(0, 1), (1, 0)])  7.82 us
    ppermute x9, starting transfers between devices, toward(): return lax.ppermute(value, ('ctx', 'doc'), pairs)  7.39 us
    pallas_call x3, Pallas kernels, products(): pl.pallas_call(body, out_shape=[jax.ShapeDtypeStruct((rows, cols), F32 if...  6.91 us
    ppermute x3, waiting for transfers between devices, hop(): return lax.ppermute(value, 'doc', pairs)  5.58 us
    ppermute x3, starting transfers between devices, hop(): return lax.ppermute(value, 'doc', pairs)  4.49 us
    ppermute x2, waiting for transfers between devices, toward(): return lax.ppermute(value, ('ctx', 'head'), pairs)  4.44 us
  transfers between devices with their start and end apart: 23, of which 18 were waited for; matrix products, arithmetic and copies ran while one was open for 2% of the time, Pallas kernels for 6%

commit v1 on v0

v1 whole, which is shorter than its diff:
```python
import math

import jax
import jax.numpy as jnp
from jax import lax
from jax.experimental import pallas as pl
from jax.experimental.pallas import tpu as pltpu
from jax.sharding import PartitionSpec as P

HEAD_SIZE = 128
BLOCK_TOKENS = 128
NKB_DEV = 32
GROUP = 8
CAP = 12
PICKS = 16
QB = 2
NX = 4
NY = 4
NZ = 8
SLOTS = QB * CAP
SENT = 2 * SLOTS + GROUP
SCALE = HEAD_SIZE**-0.5 * math.log2(math.e)
BF16 = jnp.bfloat16
F32 = jnp.float32
ANY = pl.BlockSpec(memory_space=pl.ANY)


def hop(value, step):
    pairs = [(z * NY + y, z * NY + (y + step) % NY) for z in range(NZ) for y in range(NY)]
    return lax.ppermute(value, "doc", pairs)


def toward(value, axis):
    pairs = []
    if axis == "x":
        for c, step in ((0, 1), (1, -1)):
            pairs += [(c * NX + x, c * NX + (x + step) % NX) for x in range(NX)]
        return lax.ppermute(value, ("ctx", "head"), pairs)
    for c, step in ((0, 1), (1, -1)):
        for z in range(NZ):
            for y in range(NY):
                to_z = (z + step) % NZ if axis == "z" else z
                to_y = (y + step) % NY if axis == "y" else y
                pairs.append(((c * NZ + z) * NY + y, (c * NZ + to_z) * NY + to_y))
    return lax.ppermute(value, ("ctx", "doc"), pairs)


def swap(value):
    return lax.ppermute(value, "ctx", [(0, 1), (1, 0)])


def pack_kernel(away, pattern, q, k, v, packed, sem):
    c = lax.axis_index("ctx")
    head = 1 - c if away else c
    cols = pl.ds(pl.multiple_of(head * HEAD_SIZE, HEAD_SIZE), HEAD_SIZE)
    for g in range(GROUP):
        at = pl.multiple_of(head * GROUP * HEAD_SIZE + g * HEAD_SIZE, HEAD_SIZE)
        pltpu.make_async_copy(q.at[:, pl.ds(at, HEAD_SIZE)], packed.at[2 * SLOTS + g], sem).start()
    many = 0
    for b in range(QB):
        count = 0
        for s in range(PICKS):
            block = pattern[b, s]
            mine = block // NKB_DEV == c
            row = pl.multiple_of((block % NKB_DEV) * BLOCK_TOKENS, BLOCK_TOKENS)
            slot = b * CAP + count

            @pl.when(mine)
            def _(row=row, slot=slot):
                rows = pl.ds(row, BLOCK_TOKENS)
                pltpu.make_async_copy(k.at[rows, cols], packed.at[slot], sem).start()
                pltpu.make_async_copy(v.at[rows, cols], packed.at[SLOTS + slot], sem).start()

            count = count + mine.astype(jnp.int32)
        many = many + count

    queries = packed.at[pl.ds(2 * SLOTS, GROUP)]
    pltpu.make_async_copy(queries, queries, sem).wait()

    def settle(_, carry):
        pair = packed.at[pl.ds(0, 2)]
        pltpu.make_async_copy(pair, pair, sem).wait()
        return carry

    lax.fori_loop(0, many, settle, 0)


def pack(away, pattern, q, k, v):
    def body(*refs):
        pack_kernel(away, *refs)

    return pl.pallas_call(
        body,
        out_shape=jax.ShapeDtypeStruct((SENT, BLOCK_TOKENS, HEAD_SIZE), BF16),
        in_specs=[pl.BlockSpec(memory_space=pltpu.SMEM), ANY, ANY, ANY],
        out_specs=pl.BlockSpec(memory_space=pltpu.VMEM),
        scratch_shapes=[pltpu.SemaphoreType.DMA],
        name="pack_away" if away else "pack_here",
    )(pattern, q, k, v)


def attend_kernel(pattern, kept, got, out, turned, qs, ks, vs):
    c = lax.axis_index("ctx")
    for b in range(QB):
        count = 0
        for s in range(PICKS):
            count = count + (pattern[b, s] // NKB_DEV == c).astype(jnp.int32)
        for kind, chosen in enumerate((ks, vs)):
            slots = pl.ds(kind * SLOTS + b * CAP, CAP)
            chosen[b, pl.ds(0, CAP)] = kept[slots]
            chosen[b, pl.ds(count, CAP)] = got[slots]
        for source, here in ((kept, c == b), (got, c != b)):

            @pl.when(here)
            def _(source=source, b=b):
                qs[b] = source[pl.ds(2 * SLOTS, GROUP)]

    for b in range(QB):
        keys = ks[b, :PICKS].reshape(PICKS * BLOCK_TOKENS, HEAD_SIZE)
        vals = vs[b, :PICKS].reshape(PICKS * BLOCK_TOKENS, HEAD_SIZE)
        for pair in range(GROUP // 2):
            rows = qs[b, 2 * pair : 2 * pair + 2].reshape(2 * BLOCK_TOKENS, HEAD_SIZE)
            scores = lax.dot_general(rows, keys, (((1,), (1,)), ((), ())), preferred_element_type=F32)
            top = jnp.max(scores, axis=-1, keepdims=True)
            weights = jnp.exp2((scores - top) * SCALE)
            total = jnp.sum(weights, axis=-1, keepdims=True)
            mixed = jnp.dot(weights.astype(BF16), vals, preferred_element_type=F32) / total
            for i in range(2):
                g = 2 * pair + i
                part = mixed[i * BLOCK_TOKENS : (i + 1) * BLOCK_TOKENS]
                cols = pl.ds(g * HEAD_SIZE, HEAD_SIZE)
                out[jnp.where(c == b, 0, 1), :, cols] = part.astype(BF16)
                turned[cols, pl.ds(b * BLOCK_TOKENS, BLOCK_TOKENS)] = part.T.astype(BF16)


def attend(pattern, kept, got):
    width = GROUP * HEAD_SIZE
    out = jax.ShapeDtypeStruct((QB, BLOCK_TOKENS, width), BF16)
    chosen = pltpu.VMEM((QB, 2 * CAP, BLOCK_TOKENS, HEAD_SIZE), BF16)
    vmem = pl.BlockSpec(memory_space=pltpu.VMEM)
    return pl.pallas_call(
        attend_kernel,
        out_shape=(out, jax.ShapeDtypeStruct((width, QB * BLOCK_TOKENS), BF16)),
        in_specs=[pl.BlockSpec(memory_space=pltpu.SMEM), vmem, vmem],
        out_specs=(vmem, vmem),
        scratch_shapes=[
            pltpu.VMEM((QB, GROUP, BLOCK_TOKENS, HEAD_SIZE), BF16),
            chosen,
            chosen,
        ],
        compiler_params=pltpu.CompilerParams(vmem_limit_bytes=32 << 20),
        name="attend",
    )(pattern, kept, got)


def product_kernel(tasks, *refs):
    lefts = refs[:4], refs[4:8]
    rights = tuple(zip(refs[8:12], refs[12:16]))
    outs, bt = refs[16:-1], refs[-1]
    c, x = lax.axis_index("ctx"), lax.axis_index("head")
    z = lax.axis_index("doc") // NY
    for i in sorted({i for i, _ in tasks}):
        owner = lax.rem(z + jnp.where(c == 0, 4 - i, 4 + i), NZ)
        away = lax.rem(owner // 2 + NX - x, NX)
        other = (lax.rem(owner, 2) != c).astype(jnp.int32)
        side = jnp.where(c == 0, 3, 1)
        case = jnp.where(away == 0, 0, jnp.where(away == 2, 3, jnp.where(away == side, 1, 2)))
        for k in range(4):
            for r in range(2):

                @pl.when(jnp.logical_and(case == k, other == r))
                def _(k=k, r=r):
                    bt[...] = rights[k][r][...]

        for r in sorted({r for j, r in tasks if j == i}):
            total = None
            for left, doc in zip(lefts[r], (0, 1 + c, 2 - c, 3)):
                dims = (((1,), (1,)), ((), ()))
                term = lax.dot_general(left[...], bt[doc], dims, preferred_element_type=F32)
                total = term if total is None else total + term
            out = outs[tasks.index((i, r))]
            out[...] = total.astype(out.dtype)


def products(tasks, lefts, rights):
    rows, cols = GROUP * HEAD_SIZE, 2 * HEAD_SIZE
    vmem = pl.BlockSpec(memory_space=pltpu.VMEM)

    def body(*refs):
        product_kernel(tasks, *refs)

    return pl.pallas_call(
        body,
        out_shape=[jax.ShapeDtypeStruct((rows, cols), F32 if i == 4 else BF16) for i, _ in tasks],
        in_specs=[vmem] * 16,
        out_specs=[vmem] * len(tasks),
        scratch_shapes=[pltpu.VMEM((NY, cols, QB * BLOCK_TOKENS), BF16)],
        compiler_params=pltpu.CompilerParams(vmem_limit_bytes=16 << 20),
        name="products",
    )(*lefts[0], *lefts[1], *rights[0], *rights[1])


def added(got, here):
    return (got.astype(F32) + here.astype(F32)).astype(BF16)


def per_device(queries, keys, values, pattern):
    c = lax.axis_index("ctx")
    y = lax.axis_index("doc") % NY
    q, k, v, chosen = queries[0], keys[0], values[0], pattern[0]
    got = swap(pack(True, chosen, q, k, v))
    kept = pack(False, chosen, q, k, v)
    out, turned = attend(chosen, kept, got)
    cols = 2 * HEAD_SIZE

    def share(step):
        return lax.dynamic_slice_in_dim(turned, ((y + step) % NY) * cols, cols, 0)

    mine = jnp.stack([share(0), hop(share(1), 1), hop(share(-1), -1), hop(share(2), 2)])
    x1 = toward(mine, "x")
    y1 = toward(turned, "y")
    mine_other, turned_other = swap(mine), swap(turned)
    x1_other, y1_other = toward(mine_other, "x"), toward(turned_other, "y")
    x2, y2 = toward(x1, "x"), toward(y1, "y")
    lefts = [turned, y1, swap(y1_other), y2], [turned_other, y1_other, swap(y1), swap(y2)]
    rights = [mine, x1, swap(x1_other), x2], [mine_other, x1_other, swap(x1), swap(x2)]

    [first] = products([(0, 0)], lefts, rights)
    second = products([(1, 0), (1, 1)], lefts, rights)
    third = products([(2, 0), (2, 1), (3, 0), (3, 1), (4, 0)], lefts, rights)
    long = toward(first, "z")
    short = toward(second[1], "z")
    long = toward(added(long, second[0]), "z")
    short = toward(added(short, third[1]), "z")
    long = toward(added(long, third[0]), "z")
    short = toward(added(short, third[3]), "z")
    long = toward(added(long, third[2]), "z")
    gram = third[4] + swap(short).astype(F32) + long.astype(F32)

    own, returned = out[0], swap(out[1])
    attended = jnp.where(
        c == 0,
        jnp.concatenate([own, returned], axis=1),
        jnp.concatenate([returned, own], axis=1),
    )
    return (attended[None], gram)


def solution(mesh):
    placed = (
        P("doc", "ctx", "head"),
        P("doc", "ctx", "head"),
        P("doc", "ctx", "head"),
        P("doc", None, None),
    )
    return jax.shard_map(
        per_device,
        mesh=mesh,
        in_specs=placed,
        out_specs=(P("doc", "ctx", "head"), P(("head", "ctx"), "doc")),
        check_vma=False,
    )
```

time: 109 us -> 101 us (0.927)
  waiting for transfers between devices: 67.7 us -> 55 us
  starting transfers between devices: 15.8 us -> 19.4 us
  Pallas kernels: 19 us -> 20.9 us
    ppermute x9 -> x10, waiting for transfers between devices: 49.8 us -> 38.7 us  [toward(): return lax.ppermute(value, ('ctx', 'doc'), pairs)]
    ppermute x9 -> x11, waiting for transfers between devices: 7.82 us -> 3.95 us  [swap(): return lax.ppermute(value, 'ctx', [(0, 1), (1, 0)])]
    ppermute x2 -> x3, waiting for transfers between devices: 4.44 us -> 8.05 us  [toward(): return lax.ppermute(value, ('ctx', 'head'), pairs)]
    pallas_call x1 -> x2, Pallas kernels: 3.34 us -> 6.71 us  [pack(): pl.pallas_call(body, out_shape=jax.ShapeDtypeStruct((SENT, BLOCK_TOKENS,...]
    ppermute x9 -> x10, starting transfers between devices: 7.39 us -> 8.89 us  [toward(): return lax.ppermute(value, ('ctx', 'doc'), pairs)]
    pallas_call x1, Pallas kernels: 8.77 us -> 7.28 us  [attend(): pl.pallas_call(attend_kernel, out_shape=(out, jax.ShapeDtypeStruct((width...]
    ppermute x2 -> x3, starting transfers between devices: 1.94 us -> 3.35 us  [toward(): return lax.ppermute(value, ('ctx', 'head'), pairs)]
    ppermute x3, waiting for transfers between devices: 5.58 us -> 4.32 us  [hop(): return lax.ppermute(value, 'doc', pairs)]
  transfers between devices with their start and end apart: 23 -> 27, of which waited for: 18 -> 18; matrix products, arithmetic and copies ran while one was open for 2% -> 2% of each run, Pallas kernels for 6% -> 10%
where the time goes in v1:
time: 101 us
  waiting for transfers between devices  55 us (54%)
  Pallas kernels  20.9 us (21%)
  starting transfers between devices  19.4 us (19%)
  other arithmetic  2.75 us (3%)
  local copies, waits for them, and re-layouts  1.59 us (2%)
    ppermute x10, waiting for transfers between devices, toward(): return lax.ppermute(value, ('ctx', 'doc'), pairs)  38.7 us
    ppermute x10, starting transfers between devices, toward(): return lax.ppermute(value, ('ctx', 'doc'), pairs)  8.89 us
    ppermute x3, waiting for transfers between devices, toward(): return lax.ppermute(value, ('ctx', 'head'), pairs)  8.05 us
    pallas_call x1, Pallas kernels, attend(): pl.pallas_call(attend_kernel, out_shape=(out, jax.ShapeDtypeStruct((width...  7.28 us
    pallas_call x3, Pallas kernels, products(): pl.pallas_call(body, out_shape=[jax.ShapeDtypeStruct((rows, cols), F32 if...  6.9 us
    pallas_call x2, Pallas kernels, pack(): pl.pallas_call(body, out_shape=jax.ShapeDtypeStruct((SENT, BLOCK_TOKENS,...  6.71 us
    ppermute x3, waiting for transfers between devices, hop(): return lax.ppermute(value, 'doc', pairs)  4.32 us
    ppermute x3, starting transfers between devices, hop(): return lax.ppermute(value, 'doc', pairs)  4.25 us
  transfers between devices with their start and end apart: 27, of which 18 were waited for; matrix products, arithmetic and copies ran while one was open for 2% of the time, Pallas kernels for 10%

profile of v1, /device:TPU:8, one launch (start us, length us, event | category | flops | bytes accessed | tf_op | source)
XLA Modules:
  0.0 100.6 jit_solution(3820321676198509541)
XLA Ops:
  0.6 3.3 %pack_away.1 = bf16[56,128,128]{2,1,0:T(8,128)(2,1)} custom-call(s32[2,16]{1,0:T(2,128)} %bitcast.12, bf16[128,2048]{1,0:T(8,128)(2,1)} %bitcast.19, bf16[4096,256]{1,0:T(8,128)(2,1)} %bitcast.15, bf16[4096,256]{1,0:T(8,128)(2,1)} %bitcast.17), custom_call_target="tpu_custom_call" | custom-call | tf_op jit(solution)/shard_map/pack_away/pallas_call | solution.py:92
  4.1 3.4 %pack_here.1.kept = bf16[56,128,128]{2,1,0:T(8,128)(2,1)} custom-call(s32[2,16]{1,0:T(2,128)} %bitcast.13, bf16[128,2048]{1,0:T(8,128)(2,1)} %bitcast.20, bf16[4096,256]{1,0:T(8,128)(2,1)} %bitcast.16, bf16[4096,256]{1,0:T(8,128)(2,1)} %bitcast.18), custom_call_target="tpu_custom_call" | custom-call | tf_op jit(solution)/shard_map/pack_here/pallas_call | solution.py:92
  8.0 1.5 %copy-done = bf16[56,128,128]{2,1,0:T(8,128)(2,1)S(1)} copy-done((bf16[56,128,128]{2,1,0:T(8,128)(2,1)S(1)}, bf16[56,128,128]{2,1,0:T(8,128)(2,1)}, u32[]{:S(2)}) %copy-start) | copy-done | bytes 1835032
  9.5 7.3 %attend.1 = (bf16[2,128,1024]{2,1,0:T(8,128)(2,1)S(1)}, bf16[1024,256]{1,0:T(8,128)(2,1)S(1)}) custom-call(s32[2,16]{1,0:T(2,128)S(1)} %bitcast.14, bf16[56,128,128]{2,1,0:T(8,128)(2,1)S(1)} %copy-done, bf16[56,128,128]{2,1,0:T(8,128)(2,1)S(1)} %collective-permute-done.got), custom_call_target="tpu_custom_call" | custom-call | tf_op jit(solution)/shard_map/attend/pallas_call | solution.py:141
  16.8 2.2 %collective-permute-start.11 = (bf16[256,256]{1,0:T(8,128)(2,1)S(1)}, bf16[256,256]{1,0:T(8,128)(2,1)S(1)}, u32[]{:S(2)}, u32[]{:S(2)}) collective-permute-start(bf16[256,256]{1,0:T(8,128)(2,1)S(1)} %get-tuple-element.21), channel_id=1, source_target_pairs={{0,2},{1,3},{2,0},{3,1},{4,6},{5,7},{6,4},{7,5},{8,10},{9,11},{10,... | collective-permute-start | bytes 393224 | tf_op jit(solution)/shard_map/ppermute | solution.py:30
  19.1 1.5 %collective-permute-start.10 = (bf16[256,256]{1,0:T(8,128)(2,1)S(1)}, bf16[256,256]{1,0:T(8,128)(2,1)S(1)}, u32[]{:S(2)}, u32[]{:S(2)}) collective-permute-start(bf16[256,256]{1,0:T(8,128)(2,1)S(1)} %get-tuple-element.22), channel_id=1, source_target_pairs={{0,3},{1,0},{2,1},{3,2},{4,7},{5,4},{6,5},{7,6},{8,11},{9,8},{10,9... | collective-permute-start | bytes 393224 | tf_op jit(solution)/shard_map/ppermute | solution.py:30
  21.1 1.5 %collective-permute-start.2 = (bf16[1024,256]{1,0:T(8,128)(2,1)S(1)}, bf16[1024,256]{1,0:T(8,128)(2,1)S(1)}, u32[]{:S(2)}, u32[]{:S(2)}) collective-permute-start(bf16[1024,256]{1,0:T(8,128)(2,1)S(1)} %get-tuple-element.12.refs_0_), channel_id=1, source_target_pairs={{0,1},{1,2},{2,3},{3,0},{4,5},{5,6},{6,7},{7,4},{8,9},{9,10},{10,1... | collective-permute-start | bytes 1572872 | tf_op jit(solution)/shard_map/ppermute | solution.py:45
  22.6 2.2 %collective-permute-done.11 = bf16[256,256]{1,0:T(8,128)(2,1)S(1)} collective-permute-done((bf16[256,256]{1,0:T(8,128)(2,1)S(1)}, bf16[256,256]{1,0:T(8,128)(2,1)S(1)}, u32[]{:S(2)}, u32[]{:S(2)}) %collective-permute-start.11) | collective-permute-done | bytes 131104 | tf_op jit(solution)/shard_map/ppermute | solution.py:30
  24.8 2.1 %collective-permute-done.10 = bf16[256,256]{1,0:T(8,128)(2,1)S(1)} collective-permute-done((bf16[256,256]{1,0:T(8,128)(2,1)S(1)}, bf16[256,256]{1,0:T(8,128)(2,1)S(1)}, u32[]{:S(2)}, u32[]{:S(2)}) %collective-permute-start.10) | collective-permute-done | bytes 131104 | tf_op jit(solution)/shard_map/ppermute | solution.py:30
  27.2 1.6 %collective-permute-start.12 = (bf16[4,256,256]{2,1,0:T(8,128)(2,1)S(1)}, bf16[4,256,256]{2,1,0:T(8,128)(2,1)S(1)}, u32[]{:S(2)}, u32[]{:S(2)}) collective-permute-start(bf16[4,256,256]{2,1,0:T(8,128)(2,1)S(1)} %pad_maximum_fusion.refs_8_), channel_id=1, source_target_pairs={{0,32},{32,64},{64,96},{96,0},{128,224},{160,128},{192,160},{224,1... | collective-permute-start | bytes 1572872 | tf_op jit(solution)/shard_map/ppermute | solution.py:38
  28.8 1.4 %collective-permute-start.4 = (bf16[1024,256]{1,0:T(8,128)(2,1)S(1)}, bf16[1024,256]{1,0:T(8,128)(2,1)S(1)}, u32[]{:S(2)}, u32[]{:S(2)}) collective-permute-start(bf16[1024,256]{1,0:T(8,128)(2,1)S(1)} %collective-permute-done.3.refs_4_), channel_id=1, source_target_pairs={{0,1},{1,2},{2,3},{3,0},{4,5},{5,6},{6,7},{7,4},{8,9},{9,10},{10,1... | collective-permute-start | bytes 1572872 | tf_op jit(solution)/shard_map/ppermute | solution.py:45
  30.2 2.2 %collective-permute-done.2.refs_1_ = bf16[1024,256]{1,0:T(8,128)(2,1)S(1)} collective-permute-done((bf16[1024,256]{1,0:T(8,128)(2,1)S(1)}, bf16[1024,256]{1,0:T(8,128)(2,1)S(1)}, u32[]{:S(2)}, u32[]{:S(2)}) %collective-permute-start.2) | collective-permute-done | bytes 524320 | tf_op jit(solution)/shard_map/ppermute | solution.py:45
  32.5 1.4 %collective-permute-start.6 = (bf16[1024,256]{1,0:T(8,128)(2,1)S(1)}, bf16[1024,256]{1,0:T(8,128)(2,1)S(1)}, u32[]{:S(2)}, u32[]{:S(2)}) collective-permute-start(bf16[1024,256]{1,0:T(8,128)(2,1)S(1)} %collective-permute-done.2.refs_1_), channel_id=1, source_target_pairs={{0,1},{1,2},{2,3},{3,0},{4,5},{5,6},{6,7},{7,4},{8,9},{9,10},{10,1... | collective-permute-start | bytes 1572872 | tf_op jit(solution)/shard_map/ppermute | solution.py:45
  33.9 1.5 %collective-permute-start.14 = (bf16[4,256,256]{2,1,0:T(8,128)(2,1)S(1)}, bf16[4,256,256]{2,1,0:T(8,128)(2,1)S(1)}, u32[]{:S(2)}, u32[]{:S(2)}) collective-permute-start(bf16[4,256,256]{2,1,0:T(8,128)(2,1)S(1)} %collective-permute-done.13.refs_12_), channel_id=1, source_target_pairs={{0,32},{32,64},{64,96},{96,0},{128,224},{160,128},{192,160},{224,1... | collective-permute-start | bytes 1572872 | tf_op jit(solution)/shard_map/ppermute | solution.py:38
  35.4 2.3 %collective-permute-done.12.refs_9_ = bf16[4,256,256]{2,1,0:T(8,128)(2,1)S(1)} collective-permute-done((bf16[4,256,256]{2,1,0:T(8,128)(2,1)S(1)}, bf16[4,256,256]{2,1,0:T(8,128)(2,1)S(1)}, u32[]{:S(2)}, u32[]{:S(2)}) %collective-permute-start.12) | collective-permute-done | bytes 524320 | tf_op jit(solution)/shard_map/ppermute | solution.py:38
  38.1 1.4 %collective-permute-start.17 = (bf16[4,256,256]{2,1,0:T(8,128)(2,1)S(1)}, bf16[4,256,256]{2,1,0:T(8,128)(2,1)S(1)}, u32[]{:S(2)}, u32[]{:S(2)}) collective-permute-start(bf16[4,256,256]{2,1,0:T(8,128)(2,1)S(1)} %collective-permute-done.12.refs_9_), channel_id=1, source_target_pairs={{0,128},{128,0},{1,129},{129,1},{2,130},{130,2},{3,131},{131,3},{4... | collective-permute-start | bytes 1572872 | tf_op jit(solution)/shard_map/ppermute | solution.py:49
  39.6 4.2 %collective-permute-done.6.refs_3_ = bf16[1024,256]{1,0:T(8,128)(2,1)S(1)} collective-permute-done((bf16[1024,256]{1,0:T(8,128)(2,1)S(1)}, bf16[1024,256]{1,0:T(8,128)(2,1)S(1)}, u32[]{:S(2)}, u32[]{:S(2)}) %collective-permute-start.6) | collective-permute-done | bytes 524320 | tf_op jit(solution)/shard_map/ppermute | solution.py:45
  44.3 5.6 %collective-permute-done.16.refs_11_ = bf16[4,256,256]{2,1,0:T(8,128)(2,1)S(1)} collective-permute-done((bf16[4,256,256]{2,1,0:T(8,128)(2,1)S(1)}, bf16[4,256,256]{2,1,0:T(8,128)(2,1)S(1)}, u32[]{:S(2)}, u32[]{:S(2)}) %collective-permute-start.16) | collective-permute-done | bytes 524320 | tf_op jit(solution)/shard_map/ppermute | solution.py:38
  50.0 1.9 %collective-permute-done.18.refs_15_ = bf16[4,256,256]{2,1,0:T(8,128)(2,1)S(1)} collective-permute-done((bf16[4,256,256]{2,1,0:T(8,128)(2,1)S(1)}, bf16[4,256,256]{2,1,0:T(8,128)(2,1)S(1)}, u32[]{:S(2)}, u32[]{:S(2)}) %collective-permute-start.18) | collective-permute-done | bytes 524320 | tf_op jit(solution)/shard_map/ppermute | solution.py:49
  52.6 2.0 %collective-permute-start.23 = (bf16[1024,256]{1,0:T(8,128)(2,1)S(1)}, bf16[1024,256]{1,0:T(8,128)(2,1)S(1)}, u32[]{:S(2)}, u32[]{:S(2)}) collective-permute-start(bf16[1024,256]{1,0:T(8,128)(2,1)S(1)} %products.5), channel_id=1, source_target_pairs={{0,4},{1,5},{2,6},{3,7},{4,8},{5,9},{6,10},{7,11},{8,12},{9,13},{1... | collective-permute-start | bytes 1572872 | tf_op jit(solution)/shard_map/ppermute | solution.py:45
  54.7 1.3 %products.4 = (bf16[1024,256]{1,0:T(8,128)(2,1)S(1)}, bf16[1024,256]{1,0:T(8,128)(2,1)S(1)}) custom-call(bf16[1024,256]{1,0:T(8,128)(2,1)S(1)} %get-tuple-element.12.refs_0_, bf16[1024,256]{1,0:T(8,128)(2,1)S(1)} %collective-permute-done.2.refs_1_, bf16[1024,256]{1,0:T(8,128)(2,1)S(1)} %collective-permute-done.5.refs_2_, ...), custom_call_target="tpu_custom_call" | custom-call | tf_op jit(solution)/shard_map/products/pallas_call | solution.py:192
  56.0 2.1 %collective-permute-start.19 = (bf16[1024,256]{1,0:T(8,128)(2,1)S(1)}, bf16[1024,256]{1,0:T(8,128)(2,1)S(1)}, u32[]{:S(2)}, u32[]{:S(2)}) collective-permute-start(bf16[1024,256]{1,0:T(8,128)(2,1)S(1)} %get-tuple-element.14), channel_id=1, source_target_pairs={{0,4},{1,5},{2,6},{3,7},{4,8},{5,9},{6,10},{7,11},{8,12},{9,13},{1... | collective-permute-start | bytes 1572872 | tf_op jit(solution)/shard_map/ppermute | solution.py:45
  58.1 7.6 %collective-permute-done.23 = bf16[1024,256]{1,0:T(8,128)(2,1)S(1)} collective-permute-done((bf16[1024,256]{1,0:T(8,128)(2,1)S(1)}, bf16[1024,256]{1,0:T(8,128)(2,1)S(1)}, u32[]{:S(2)}, u32[]{:S(2)}) %collective-permute-start.23) | collective-permute-done | bytes 524320 | tf_op jit(solution)/shard_map/ppermute | solution.py:45
  66.0 4.8 %products.3 = (bf16[1024,256]{1,0:T(8,128)(2,1)S(1)}, bf16[1024,256]{1,0:T(8,128)(2,1)S(1)}, bf16[1024,256]{1,0:T(8,128)(2,1)S(1)}, bf16[1024,256]{1,0:T(8,128)(2,1)S(1)}, f32[1024,256]{1,0:T(8,128)S(1)}) custom-call(bf16[1024,256]{1,0:T(8,128)(2,1)S(1)} %get-tuple-element.12.refs_0_, bf16[1024,256]{1,0:T(8,128)(2,1)S(1)} %collective-permute-done.2.refs_1_, ...), custom_call_target="tpu_custom_call" | custom-call | tf_op jit(solution)/shard_map/products/pallas_call | solution.py:192
  71.6 5.4 %collective-permute-done.24 = bf16[1024,256]{1,0:T(8,128)(2,1)S(1)} collective-permute-done((bf16[1024,256]{1,0:T(8,128)(2,1)S(1)}, bf16[1024,256]{1,0:T(8,128)(2,1)S(1)}, u32[]{:S(2)}, u32[]{:S(2)}) %collective-permute-start.24) | collective-permute-done | bytes 524320 | tf_op jit(solution)/shard_map/ppermute | solution.py:45
  77.2 5.4 %collective-permute-done.20 = bf16[1024,256]{1,0:T(8,128)(2,1)S(1)} collective-permute-done((bf16[1024,256]{1,0:T(8,128)(2,1)S(1)}, bf16[1024,256]{1,0:T(8,128)(2,1)S(1)}, u32[]{:S(2)}, u32[]{:S(2)}) %collective-permute-start.20) | collective-permute-done | bytes 524320 | tf_op jit(solution)/shard_map/ppermute | solution.py:45
  82.8 5.4 %collective-permute-done.25 = bf16[1024,256]{1,0:T(8,128)(2,1)S(1)} collective-permute-done((bf16[1024,256]{1,0:T(8,128)(2,1)S(1)}, bf16[1024,256]{1,0:T(8,128)(2,1)S(1)}, u32[]{:S(2)}, u32[]{:S(2)}) %collective-permute-start.25) | collective-permute-done | bytes 524320 | tf_op jit(solution)/shard_map/ppermute | solution.py:45
  88.5 5.5 %collective-permute-done.21 = bf16[1024,256]{1,0:T(8,128)(2,1)} collective-permute-done((bf16[1024,256]{1,0:T(8,128)(2,1)S(1)}, bf16[1024,256]{1,0:T(8,128)(2,1)}, u32[]{:S(2)}, u32[]{:S(2)}) %collective-permute-start.21) | collective-permute-done | bytes 524320 | tf_op jit(solution)/shard_map/ppermute | solution.py:45
  94.6 1.6 %collective-permute-done.1 = bf16[128,1024]{1,0:T(8,128)(2,1)S(1)} collective-permute-done((bf16[128,1024]{1,0:T(8,128)(2,1)S(1)}, bf16[128,1024]{1,0:T(8,128)(2,1)S(1)}, u32[]{:S(2)}, u32[]{:S(2)}) %collective-permute-start.1) | collective-permute-done | bytes 262176 | tf_op jit(solution)/shard_map/ppermute | solution.py:49
  96.2 0.9 maximum_select_fusion
  97.2 2.3 %collective-permute-done.26 = bf16[1024,256]{1,0:T(8,128)(2,1)S(1)} collective-permute-done((bf16[1024,256]{1,0:T(8,128)(2,1)S(1)}, bf16[1024,256]{1,0:T(8,128)(2,1)S(1)}, u32[]{:S(2)}, u32[]{:S(2)}) %collective-permute-start.26) | collective-permute-done | bytes 524320 | tf_op jit(solution)/shard_map/ppermute | solution.py:45
  99.5 1.1 %convert_add_fusion = f32[1024,256]{1,0:T(8,128)} fusion(bf16[1024,256]{1,0:T(8,128)(2,1)S(1)} %collective-permute-done.26, f32[1024,256]{1,0:T(8,128)S(1)} %get-tuple-element.13, bf16[1024,256]{1,0:T(8,128)(2,1)S(1)} %collective-permute-done.22), kind=kLoop, calls=%fused_computation | loop fusion | flops 1048576 | bytes 3145728 | tf_op jit(solution)/shard_map/add | solution.py:238
  (42 shorter events, 5.7 us)
Async XLA Ops:
  3.9 4.1 %collective-permute-start = (bf16[56,128,128]{2,1,0:T(8,128)(2,1)}, bf16[56,128,128]{2,1,0:T(8,128)(2,1)S(1)}, u32[]{:S(2)}, u32[]{:S(2)}) collective-permute-start(bf16[56,128,128]{2,1,0:T(8,128)(2,1)} %pack_away.1), channel_id=1, source_target_pairs={{0,128},{128,0},{1,129},{129,1},{2,130},{130,2},{3,131},{131,3},{4... | collective-permute-start | bytes 5505032 | tf_op jit(solution)/shard_map/ppermute | solution.py:49
  4.1 3.9 %copy-start.1 = (s32[1,2,16]{2,1,0:T(2,128)S(1)}, s32[1,2,16]{2,1,0:T(2,128)}, u32[]{:S(2)}) copy-start(s32[1,2,16]{2,1,0:T(2,128)} %param.7) | copy-start | bytes 388
  8.0 1.5 %copy-start = (bf16[56,128,128]{2,1,0:T(8,128)(2,1)S(1)}, bf16[56,128,128]{2,1,0:T(8,128)(2,1)}, u32[]{:S(2)}) copy-start(bf16[56,128,128]{2,1,0:T(8,128)(2,1)} %pack_here.1.kept) | copy-start | bytes 5505028
  16.8 8.0 %collective-permute-start.11 = (bf16[256,256]{1,0:T(8,128)(2,1)S(1)}, bf16[256,256]{1,0:T(8,128)(2,1)S(1)}, u32[]{:S(2)}, u32[]{:S(2)}) collective-permute-start(bf16[256,256]{1,0:T(8,128)(2,1)S(1)} %get-tuple-element.21), channel_id=1, source_target_pairs={{0,2},{1,3},{2,0},{3,1},{4,6},{5,7},{6,4},{7,5},{8,10},{9,11},{10,... | collective-permute-start | bytes 393224 | tf_op jit(solution)/shard_map/ppermute | solution.py:30
  19.1 7.8 %collective-permute-start.10 = (bf16[256,256]{1,0:T(8,128)(2,1)S(1)}, bf16[256,256]{1,0:T(8,128)(2,1)S(1)}, u32[]{:S(2)}, u32[]{:S(2)}) collective-permute-start(bf16[256,256]{1,0:T(8,128)(2,1)S(1)} %get-tuple-element.22), channel_id=1, source_target_pairs={{0,3},{1,0},{2,1},{3,2},{4,7},{5,4},{6,5},{7,6},{8,11},{9,8},{10,9... | collective-permute-start | bytes 393224 | tf_op jit(solution)/shard_map/ppermute | solution.py:30
  20.5 6.3 %collective-permute-start.9 = (bf16[256,256]{1,0:T(8,128)(2,1)S(1)}, bf16[256,256]{1,0:T(8,128)(2,1)S(1)}, u32[]{:S(2)}, u32[]{:S(2)}) collective-permute-start(bf16[256,256]{1,0:T(8,128)(2,1)S(1)} %get-tuple-element.23), channel_id=1, source_target_pairs={{0,1},{1,2},{2,3},{3,0},{4,5},{5,6},{6,7},{7,4},{8,9},{9,10},{10,1... | collective-permute-start | bytes 393224 | tf_op jit(solution)/shard_map/ppermute | solution.py:30
  21.1 7.7 %collective-permute-start.3 = (bf16[1024,256]{1,0:T(8,128)(2,1)S(1)}, bf16[1024,256]{1,0:T(8,128)(2,1)S(1)}, u32[]{:S(2)}, u32[]{:S(2)}) collective-permute-start(bf16[1024,256]{1,0:T(8,128)(2,1)S(1)} %get-tuple-element.12.refs_0_), channel_id=1, source_target_pairs={{0,128},{128,0},{1,129},{129,1},{2,130},{130,2},{3,131},{131,3},{4... | collective-permute-start | bytes 1572872 | tf_op jit(solution)/shard_map/ppermute | solution.py:49
  21.1 11.4 %collective-permute-start.2 = (bf16[1024,256]{1,0:T(8,128)(2,1)S(1)}, bf16[1024,256]{1,0:T(8,128)(2,1)S(1)}, u32[]{:S(2)}, u32[]{:S(2)}) collective-permute-start(bf16[1024,256]{1,0:T(8,128)(2,1)S(1)} %get-tuple-element.12.refs_0_), channel_id=1, source_target_pairs={{0,1},{1,2},{2,3},{3,0},{4,5},{5,6},{6,7},{7,4},{8,9},{9,10},{10,1... | collective-permute-start | bytes 1572872 | tf_op jit(solution)/shard_map/ppermute | solution.py:45
  26.9 7.0 %collective-permute-start.13 = (bf16[4,256,256]{2,1,0:T(8,128)(2,1)S(1)}, bf16[4,256,256]{2,1,0:T(8,128)(2,1)S(1)}, u32[]{:S(2)}, u32[]{:S(2)}) collective-permute-start(bf16[4,256,256]{2,1,0:T(8,128)(2,1)S(1)} %pad_maximum_fusion.refs_8_), channel_id=1, source_target_pairs={{0,128},{128,0},{1,129},{129,1},{2,130},{130,2},{3,131},{131,3},{4... | collective-permute-start | bytes 1572872 | tf_op jit(solution)/shard_map/ppermute | solution.py:49
  27.2 10.5 %collective-permute-start.12 = (bf16[4,256,256]{2,1,0:T(8,128)(2,1)S(1)}, bf16[4,256,256]{2,1,0:T(8,128)(2,1)S(1)}, u32[]{:S(2)}, u32[]{:S(2)}) collective-permute-start(bf16[4,256,256]{2,1,0:T(8,128)(2,1)S(1)} %pad_maximum_fusion.refs_8_), channel_id=1, source_target_pairs={{0,32},{32,64},{64,96},{96,0},{128,224},{160,128},{192,160},{224,1... | collective-permute-start | bytes 1572872 | tf_op jit(solution)/shard_map/ppermute | solution.py:38
  28.8 9.3 %collective-permute-start.4 = (bf16[1024,256]{1,0:T(8,128)(2,1)S(1)}, bf16[1024,256]{1,0:T(8,128)(2,1)S(1)}, u32[]{:S(2)}, u32[]{:S(2)}) collective-permute-start(bf16[1024,256]{1,0:T(8,128)(2,1)S(1)} %collective-permute-done.3.refs_4_), channel_id=1, source_target_pairs={{0,1},{1,2},{2,3},{3,0},{4,5},{5,6},{6,7},{7,4},{8,9},{9,10},{10,1... | collective-permute-start | bytes 1572872 | tf_op jit(solution)/shard_map/ppermute | solution.py:45
  32.5 7.0 %collective-permute-start.7 = (bf16[1024,256]{1,0:T(8,128)(2,1)S(1)}, bf16[1024,256]{1,0:T(8,128)(2,1)S(1)}, u32[]{:S(2)}, u32[]{:S(2)}) collective-permute-start(bf16[1024,256]{1,0:T(8,128)(2,1)S(1)} %collective-permute-done.2.refs_1_), channel_id=1, source_target_pairs={{0,128},{128,0},{1,129},{129,1},{2,130},{130,2},{3,131},{131,3},{4... | collective-permute-start | bytes 1572872 | tf_op jit(solution)/shard_map/ppermute | solution.py:49
  32.5 11.2 %collective-permute-start.6 = (bf16[1024,256]{1,0:T(8,128)(2,1)S(1)}, bf16[1024,256]{1,0:T(8,128)(2,1)S(1)}, u32[]{:S(2)}, u32[]{:S(2)}) collective-permute-start(bf16[1024,256]{1,0:T(8,128)(2,1)S(1)} %collective-permute-done.2.refs_1_), channel_id=1, source_target_pairs={{0,1},{1,2},{2,3},{3,0},{4,5},{5,6},{6,7},{7,4},{8,9},{9,10},{10,1... | collective-permute-start | bytes 1572872 | tf_op jit(solution)/shard_map/ppermute | solution.py:45
  33.9 10.4 %collective-permute-start.14 = (bf16[4,256,256]{2,1,0:T(8,128)(2,1)S(1)}, bf16[4,256,256]{2,1,0:T(8,128)(2,1)S(1)}, u32[]{:S(2)}, u32[]{:S(2)}) collective-permute-start(bf16[4,256,256]{2,1,0:T(8,128)(2,1)S(1)} %collective-permute-done.13.refs_12_), channel_id=1, source_target_pairs={{0,32},{32,64},{64,96},{96,0},{128,224},{160,128},{192,160},{224,1... | collective-permute-start | bytes 1572872 | tf_op jit(solution)/shard_map/ppermute | solution.py:38
  37.7 12.3 %collective-permute-start.16 = (bf16[4,256,256]{2,1,0:T(8,128)(2,1)S(1)}, bf16[4,256,256]{2,1,0:T(8,128)(2,1)S(1)}, u32[]{:S(2)}, u32[]{:S(2)}) collective-permute-start(bf16[4,256,256]{2,1,0:T(8,128)(2,1)S(1)} %collective-permute-done.12.refs_9_), channel_id=1, source_target_pairs={{0,32},{32,64},{64,96},{96,0},{128,224},{160,128},{192,160},{224,1... | collective-permute-start | bytes 1572872 | tf_op jit(solution)/shard_map/ppermute | solution.py:38
  38.1 11.9 %collective-permute-start.17 = (bf16[4,256,256]{2,1,0:T(8,128)(2,1)S(1)}, bf16[4,256,256]{2,1,0:T(8,128)(2,1)S(1)}, u32[]{:S(2)}, u32[]{:S(2)}) collective-permute-start(bf16[4,256,256]{2,1,0:T(8,128)(2,1)S(1)} %collective-permute-done.12.refs_9_), channel_id=1, source_target_pairs={{0,128},{128,0},{1,129},{129,1},{2,130},{130,2},{3,131},{131,3},{4... | collective-permute-start | bytes 1572872 | tf_op jit(solution)/shard_map/ppermute | solution.py:49
  39.5 10.5 %collective-permute-start.5 = (bf16[1024,256]{1,0:T(8,128)(2,1)S(1)}, bf16[1024,256]{1,0:T(8,128)(2,1)S(1)}, u32[]{:S(2)}, u32[]{:S(2)}) collective-permute-start(bf16[1024,256]{1,0:T(8,128)(2,1)S(1)} %collective-permute-done.4.refs_5_), channel_id=1, source_target_pairs={{0,128},{128,0},{1,129},{129,1},{2,130},{130,2},{3,131},{131,3},{4... | collective-permute-start | bytes 1572872 | tf_op jit(solution)/shard_map/ppermute | solution.py:49
  43.7 6.3 %collective-permute-start.8 = (bf16[1024,256]{1,0:T(8,128)(2,1)S(1)}, bf16[1024,256]{1,0:T(8,128)(2,1)S(1)}, u32[]{:S(2)}, u32[]{:S(2)}) collective-permute-start(bf16[1024,256]{1,0:T(8,128)(2,1)S(1)} %collective-permute-done.6.refs_3_), channel_id=1, source_target_pairs={{0,128},{128,0},{1,129},{129,1},{2,130},{130,2},{3,131},{131,3},{4... | collective-permute-start | bytes 1572872 | tf_op jit(solution)/shard_map/ppermute | solution.py:49
  44.3 5.6 %collective-permute-start.15 = (bf16[4,256,256]{2,1,0:T(8,128)(2,1)S(1)}, bf16[4,256,256]{2,1,0:T(8,128)(2,1)S(1)}, u32[]{:S(2)}, u32[]{:S(2)}) collective-permute-start(bf16[4,256,256]{2,1,0:T(8,128)(2,1)S(1)} %collective-permute-done.14.refs_13_), channel_id=1, source_target_pairs={{0,128},{128,0},{1,129},{129,1},{2,130},{130,2},{3,131},{131,3},{4... | collective-permute-start | bytes 1572872 | tf_op jit(solution)/shard_map/ppermute | solution.py:49
  50.0 1.9 %collective-permute-start.18 = (bf16[4,256,256]{2,1,0:T(8,128)(2,1)S(1)}, bf16[4,256,256]{2,1,0:T(8,128)(2,1)S(1)}, u32[]{:S(2)}, u32[]{:S(2)}) collective-permute-start(bf16[4,256,256]{2,1,0:T(8,128)(2,1)S(1)} %collective-permute-done.16.refs_11_), channel_id=1, source_target_pairs={{0,128},{128,0},{1,129},{129,1},{2,130},{130,2},{3,131},{131,3},{4... | collective-permute-start | bytes 1572872 | tf_op jit(solution)/shard_map/ppermute | solution.py:49
  52.6 13.1 %collective-permute-start.23 = (bf16[1024,256]{1,0:T(8,128)(2,1)S(1)}, bf16[1024,256]{1,0:T(8,128)(2,1)S(1)}, u32[]{:S(2)}, u32[]{:S(2)}) collective-permute-start(bf16[1024,256]{1,0:T(8,128)(2,1)S(1)} %products.5), channel_id=1, source_target_pairs={{0,4},{1,5},{2,6},{3,7},{4,8},{5,9},{6,10},{7,11},{8,12},{9,13},{1... | collective-permute-start | bytes 1572872 | tf_op jit(solution)/shard_map/ppermute | solution.py:45
  56.0 15.4 %collective-permute-start.19 = (bf16[1024,256]{1,0:T(8,128)(2,1)S(1)}, bf16[1024,256]{1,0:T(8,128)(2,1)S(1)}, u32[]{:S(2)}, u32[]{:S(2)}) collective-permute-start(bf16[1024,256]{1,0:T(8,128)(2,1)S(1)} %get-tuple-element.14), channel_id=1, source_target_pairs={{0,4},{1,5},{2,6},{3,7},{4,8},{5,9},{6,10},{7,11},{8,12},{9,13},{1... | collective-permute-start | bytes 1572872 | tf_op jit(solution)/shard_map/ppermute | solution.py:45
  65.9 11.1 %collective-permute-start.24 = (bf16[1024,256]{1,0:T(8,128)(2,1)S(1)}, bf16[1024,256]{1,0:T(8,128)(2,1)S(1)}, u32[]{:S(2)}, u32[]{:S(2)}) collective-permute-start(bf16[1024,256]{1,0:T(8,128)(2,1)S(1)} %add_convert_fusion.2), channel_id=1, source_target_pairs={{0,4},{1,5},{2,6},{3,7},{4,8},{5,9},{6,10},{7,11},{8,12},{9,13},{1... | collective-permute-start | bytes 1572872 | tf_op jit(solution)/shard_map/ppermute | solution.py:45
  71.5 11.1 %collective-permute-start.20 = (bf16[1024,256]{1,0:T(8,128)(2,1)S(1)}, bf16[1024,256]{1,0:T(8,128)(2,1)S(1)}, u32[]{:S(2)}, u32[]{:S(2)}) collective-permute-start(bf16[1024,256]{1,0:T(8,128)(2,1)S(1)} %add_convert_fusion.4), channel_id=1, source_target_pairs={{0,4},{1,5},{2,6},{3,7},{4,8},{5,9},{6,10},{7,11},{8,12},{9,13},{1... | collective-permute-start | bytes 1572872 | tf_op jit(solution)/shard_map/ppermute | solution.py:45
  77.1 11.1 %collective-permute-start.25 = (bf16[1024,256]{1,0:T(8,128)(2,1)S(1)}, bf16[1024,256]{1,0:T(8,128)(2,1)S(1)}, u32[]{:S(2)}, u32[]{:S(2)}) collective-permute-start(bf16[1024,256]{1,0:T(8,128)(2,1)S(1)} %add_convert_fusion.1), channel_id=1, source_target_pairs={{0,4},{1,5},{2,6},{3,7},{4,8},{5,9},{6,10},{7,11},{8,12},{9,13},{1... | collective-permute-start | bytes 1572872 | tf_op jit(solution)/shard_map/ppermute | solution.py:45
  82.8 11.2 %collective-permute-start.21 = (bf16[1024,256]{1,0:T(8,128)(2,1)S(1)}, bf16[1024,256]{1,0:T(8,128)(2,1)}, u32[]{:S(2)}, u32[]{:S(2)}) collective-permute-start(bf16[1024,256]{1,0:T(8,128)(2,1)S(1)} %add_convert_fusion.3), channel_id=1, source_target_pairs={{0,4},{1,5},{2,6},{3,7},{4,8},{5,9},{6,10},{7,11},{8,12},{9,13},{1... | collective-permute-start | bytes 1572872 | tf_op jit(solution)/shard_map/ppermute | solution.py:45
  88.4 11.1 %collective-permute-start.26 = (bf16[1024,256]{1,0:T(8,128)(2,1)S(1)}, bf16[1024,256]{1,0:T(8,128)(2,1)S(1)}, u32[]{:S(2)}, u32[]{:S(2)}) collective-permute-start(bf16[1024,256]{1,0:T(8,128)(2,1)S(1)} %add_convert_fusion), channel_id=1, source_target_pairs={{0,4},{1,5},{2,6},{3,7},{4,8},{5,9},{6,10},{7,11},{8,12},{9,13},{1... | collective-permute-start | bytes 1572872 | tf_op jit(solution)/shard_map/ppermute | solution.py:45
  94.0 5.5 %collective-permute-start.22 = (bf16[1024,256]{1,0:T(8,128)(2,1)}, bf16[1024,256]{1,0:T(8,128)(2,1)S(1)}, u32[]{:S(2)}, u32[]{:S(2)}) collective-permute-start(bf16[1024,256]{1,0:T(8,128)(2,1)} %collective-permute-done.21), channel_id=1, source_target_pairs={{0,128},{128,0},{1,129},{129,1},{2,130},{130,2},{3,131},{131,3},{4... | collective-permute-start | bytes 1572872 | tf_op jit(solution)/shard_map/ppermute | solution.py:49
  94.0 2.2 %collective-permute-start.1 = (bf16[128,1024]{1,0:T(8,128)(2,1)S(1)}, bf16[128,1024]{1,0:T(8,128)(2,1)S(1)}, u32[]{:S(2)}, u32[]{:S(2)}) collective-permute-start(bf16[128,1024]{1,0:T(8,128)(2,1)S(1)} %get-tuple-element.25), channel_id=1, source_target_pairs={{0,128},{128,0},{1,129},{129,1},{2,130},{130,2},{3,131},{131,3},{4... | collective-permute-start | bytes 786440 | tf_op jit(solution)/shard_map/ppermute | solution.py:49

commit v2 on v1

--- a/solution.py
+++ b/solution.py
@@ -230,7 +230,8 @@
     third = products([(2, 0), (2, 1), (3, 0), (3, 1), (4, 0)], lefts, rights)
     long = toward(first, "z")
     short = toward(second[1], "z")
-    long = toward(added(long, second[0]), "z")
+    here, third = lax.optimization_barrier((second[0], third))
+    long = toward(added(long, here), "z")
     short = toward(added(short, third[1]), "z")
     long = toward(added(long, third[0]), "z")
     short = toward(added(short, third[3]), "z")

time: 101 us -> 101 us (level)
  transfers between devices with their start and end apart: 27 -> 27, of which waited for: 18 -> 18; matrix products, arithmetic and copies ran while one was open for 2% -> 2% of each run, Pallas kernels for 10% -> 9%
where the time goes in v2:
time: 101 us
  waiting for transfers between devices  55.2 us (55%)
  Pallas kernels  20.6 us (20%)
  starting transfers between devices  19.5 us (19%)
  other arithmetic  2.75 us (3%)
  local copies, waits for them, and re-layouts  1.59 us (2%)
    ppermute x10, waiting for transfers between devices, toward(): return lax.ppermute(value, ('ctx', 'doc'), pairs)  39 us
    ppermute x10, starting transfers between devices, toward(): return lax.ppermute(value, ('ctx', 'doc'), pairs)  8.81 us
    ppermute x3, waiting for transfers between devices, toward(): return lax.ppermute(value, ('ctx', 'head'), pairs)  8.06 us
    pallas_call x1, Pallas kernels, attend(): pl.pallas_call(attend_kernel, out_shape=(out, jax.ShapeDtypeStruct((width...  7.3 us
    pallas_call x3, Pallas kernels, products(): pl.pallas_call(body, out_shape=[jax.ShapeDtypeStruct((rows, cols), F32 if...  6.85 us
    pallas_call x2, Pallas kernels, pack(): pl.pallas_call(body, out_shape=jax.ShapeDtypeStruct((SENT, BLOCK_TOKENS,...  6.44 us
    ppermute x3, starting transfers between devices, hop(): return lax.ppermute(value, 'doc', pairs)  4.53 us
    ppermute x11, waiting for transfers between devices, swap(): return lax.ppermute(value, 'ctx', [(0, 1), (1, 0)])  4.09 us
  transfers between devices with their start and end apart: 27, of which 18 were waited for; matrix products, arithmetic and copies ran while one was open for 2% of the time, Pallas kernels for 9%

profile of v2, /device:TPU:8, one launch (start us, length us, event | category | flops | bytes accessed | tf_op | source)
XLA Modules:
  0.0 100.6 jit_solution(7874332235583944898)
XLA Ops:
  0.6 3.1 %pack_away.1 = bf16[56,128,128]{2,1,0:T(8,128)(2,1)} custom-call(s32[2,16]{1,0:T(2,128)} %bitcast.12, bf16[128,2048]{1,0:T(8,128)(2,1)} %bitcast.19, bf16[4096,256]{1,0:T(8,128)(2,1)} %bitcast.15, bf16[4096,256]{1,0:T(8,128)(2,1)} %bitcast.17), custom_call_target="tpu_custom_call" | custom-call | tf_op jit(solution)/shard_map/pack_away/pallas_call | solution.py:92
  4.0 3.3 %pack_here.1.kept = bf16[56,128,128]{2,1,0:T(8,128)(2,1)} custom-call(s32[2,16]{1,0:T(2,128)} %bitcast.13, bf16[128,2048]{1,0:T(8,128)(2,1)} %bitcast.20, bf16[4096,256]{1,0:T(8,128)(2,1)} %bitcast.16, bf16[4096,256]{1,0:T(8,128)(2,1)} %bitcast.18), custom_call_target="tpu_custom_call" | custom-call | tf_op jit(solution)/shard_map/pack_here/pallas_call | solution.py:92
  7.9 1.5 %copy-done = bf16[56,128,128]{2,1,0:T(8,128)(2,1)S(1)} copy-done((bf16[56,128,128]{2,1,0:T(8,128)(2,1)S(1)}, bf16[56,128,128]{2,1,0:T(8,128)(2,1)}, u32[]{:S(2)}) %copy-start) | copy-done | bytes 1835032
  9.4 7.3 %attend.1 = (bf16[2,128,1024]{2,1,0:T(8,128)(2,1)S(1)}, bf16[1024,256]{1,0:T(8,128)(2,1)S(1)}) custom-call(s32[2,16]{1,0:T(2,128)S(1)} %bitcast.14, bf16[56,128,128]{2,1,0:T(8,128)(2,1)S(1)} %copy-done, bf16[56,128,128]{2,1,0:T(8,128)(2,1)S(1)} %collective-permute-done.got), custom_call_target="tpu_custom_call" | custom-call | tf_op jit(solution)/shard_map/attend/pallas_call | solution.py:141
  16.7 2.5 %collective-permute-start.11 = (bf16[256,256]{1,0:T(8,128)(2,1)S(1)}, bf16[256,256]{1,0:T(8,128)(2,1)S(1)}, u32[]{:S(2)}, u32[]{:S(2)}) collective-permute-start(bf16[256,256]{1,0:T(8,128)(2,1)S(1)} %get-tuple-element.33), channel_id=1, source_target_pairs={{0,2},{1,3},{2,0},{3,1},{4,6},{5,7},{6,4},{7,5},{8,10},{9,11},{10,... | collective-permute-start | bytes 393224 | tf_op jit(solution)/shard_map/ppermute | solution.py:30
  19.2 1.2 %collective-permute-start.10 = (bf16[256,256]{1,0:T(8,128)(2,1)S(1)}, bf16[256,256]{1,0:T(8,128)(2,1)S(1)}, u32[]{:S(2)}, u32[]{:S(2)}) collective-permute-start(bf16[256,256]{1,0:T(8,128)(2,1)S(1)} %get-tuple-element.34), channel_id=1, source_target_pairs={{0,3},{1,0},{2,1},{3,2},{4,7},{5,4},{6,5},{7,6},{8,11},{9,8},{10,9... | collective-permute-start | bytes 393224 | tf_op jit(solution)/shard_map/ppermute | solution.py:30
  21.2 1.5 %collective-permute-start.2 = (bf16[1024,256]{1,0:T(8,128)(2,1)S(1)}, bf16[1024,256]{1,0:T(8,128)(2,1)S(1)}, u32[]{:S(2)}, u32[]{:S(2)}) collective-permute-start(bf16[1024,256]{1,0:T(8,128)(2,1)S(1)} %get-tuple-element.18.refs_0_), channel_id=1, source_target_pairs={{0,1},{1,2},{2,3},{3,0},{4,5},{5,6},{6,7},{7,4},{8,9},{9,10},{10,1... | collective-permute-start | bytes 1572872 | tf_op jit(solution)/shard_map/ppermute | solution.py:45
  22.7 1.9 %collective-permute-done.11 = bf16[256,256]{1,0:T(8,128)(2,1)S(1)} collective-permute-done((bf16[256,256]{1,0:T(8,128)(2,1)S(1)}, bf16[256,256]{1,0:T(8,128)(2,1)S(1)}, u32[]{:S(2)}, u32[]{:S(2)}) %collective-permute-start.11) | collective-permute-done | bytes 131104 | tf_op jit(solution)/shard_map/ppermute | solution.py:30
  24.7 2.1 %collective-permute-done.10 = bf16[256,256]{1,0:T(8,128)(2,1)S(1)} collective-permute-done((bf16[256,256]{1,0:T(8,128)(2,1)S(1)}, bf16[256,256]{1,0:T(8,128)(2,1)S(1)}, u32[]{:S(2)}, u32[]{:S(2)}) %collective-permute-start.10) | collective-permute-done | bytes 131104 | tf_op jit(solution)/shard_map/ppermute | solution.py:30
  27.1 1.6 %collective-permute-start.12 = (bf16[4,256,256]{2,1,0:T(8,128)(2,1)S(1)}, bf16[4,256,256]{2,1,0:T(8,128)(2,1)S(1)}, u32[]{:S(2)}, u32[]{:S(2)}) collective-permute-start(bf16[4,256,256]{2,1,0:T(8,128)(2,1)S(1)} %pad_maximum_fusion.refs_8_), channel_id=1, source_target_pairs={{0,32},{32,64},{64,96},{96,0},{128,224},{160,128},{192,160},{224,1... | collective-permute-start | bytes 1572872 | tf_op jit(solution)/shard_map/ppermute | solution.py:38
  28.7 1.5 %collective-permute-start.4 = (bf16[1024,256]{1,0:T(8,128)(2,1)S(1)}, bf16[1024,256]{1,0:T(8,128)(2,1)S(1)}, u32[]{:S(2)}, u32[]{:S(2)}) collective-permute-start(bf16[1024,256]{1,0:T(8,128)(2,1)S(1)} %collective-permute-done.3.refs_4_), channel_id=1, source_target_pairs={{0,1},{1,2},{2,3},{3,0},{4,5},{5,6},{6,7},{7,4},{8,9},{9,10},{10,1... | collective-permute-start | bytes 1572872 | tf_op jit(solution)/shard_map/ppermute | solution.py:45
  30.2 2.2 %collective-permute-done.2.refs_1_ = bf16[1024,256]{1,0:T(8,128)(2,1)S(1)} collective-permute-done((bf16[1024,256]{1,0:T(8,128)(2,1)S(1)}, bf16[1024,256]{1,0:T(8,128)(2,1)S(1)}, u32[]{:S(2)}, u32[]{:S(2)}) %collective-permute-start.2) | collective-permute-done | bytes 524320 | tf_op jit(solution)/shard_map/ppermute | solution.py:45
  32.4 1.5 %collective-permute-start.6 = (bf16[1024,256]{1,0:T(8,128)(2,1)S(1)}, bf16[1024,256]{1,0:T(8,128)(2,1)S(1)}, u32[]{:S(2)}, u32[]{:S(2)}) collective-permute-start(bf16[1024,256]{1,0:T(8,128)(2,1)S(1)} %collective-permute-done.2.refs_1_), channel_id=1, source_target_pairs={{0,1},{1,2},{2,3},{3,0},{4,5},{5,6},{6,7},{7,4},{8,9},{9,10},{10,1... | collective-permute-start | bytes 1572872 | tf_op jit(solution)/shard_map/ppermute | solution.py:45
  33.9 1.5 %collective-permute-start.14 = (bf16[4,256,256]{2,1,0:T(8,128)(2,1)S(1)}, bf16[4,256,256]{2,1,0:T(8,128)(2,1)S(1)}, u32[]{:S(2)}, u32[]{:S(2)}) collective-permute-start(bf16[4,256,256]{2,1,0:T(8,128)(2,1)S(1)} %collective-permute-done.13.refs_12_), channel_id=1, source_target_pairs={{0,32},{32,64},{64,96},{96,0},{128,224},{160,128},{192,160},{224,1... | collective-permute-start | bytes 1572872 | tf_op jit(solution)/shard_map/ppermute | solution.py:38
  35.4 2.2 %collective-permute-done.12.refs_9_ = bf16[4,256,256]{2,1,0:T(8,128)(2,1)S(1)} collective-permute-done((bf16[4,256,256]{2,1,0:T(8,128)(2,1)S(1)}, bf16[4,256,256]{2,1,0:T(8,128)(2,1)S(1)}, u32[]{:S(2)}, u32[]{:S(2)}) %collective-permute-start.12) | collective-permute-done | bytes 524320 | tf_op jit(solution)/shard_map/ppermute | solution.py:38
  38.0 1.3 %collective-permute-start.17 = (bf16[4,256,256]{2,1,0:T(8,128)(2,1)S(1)}, bf16[4,256,256]{2,1,0:T(8,128)(2,1)S(1)}, u32[]{:S(2)}, u32[]{:S(2)}) collective-permute-start(bf16[4,256,256]{2,1,0:T(8,128)(2,1)S(1)} %collective-permute-done.12.refs_9_), channel_id=1, source_target_pairs={{0,128},{128,0},{1,129},{129,1},{2,130},{130,2},{3,131},{131,3},{4... | collective-permute-start | bytes 1572872 | tf_op jit(solution)/shard_map/ppermute | solution.py:49
  39.4 4.2 %collective-permute-done.6.refs_3_ = bf16[1024,256]{1,0:T(8,128)(2,1)S(1)} collective-permute-done((bf16[1024,256]{1,0:T(8,128)(2,1)S(1)}, bf16[1024,256]{1,0:T(8,128)(2,1)S(1)}, u32[]{:S(2)}, u32[]{:S(2)}) %collective-permute-start.6) | collective-permute-done | bytes 524320 | tf_op jit(solution)/shard_map/ppermute | solution.py:45
  44.2 5.6 %collective-permute-done.16.refs_11_ = bf16[4,256,256]{2,1,0:T(8,128)(2,1)S(1)} collective-permute-done((bf16[4,256,256]{2,1,0:T(8,128)(2,1)S(1)}, bf16[4,256,256]{2,1,0:T(8,128)(2,1)S(1)}, u32[]{:S(2)}, u32[]{:S(2)}) %collective-permute-start.16) | collective-permute-done | bytes 524320 | tf_op jit(solution)/shard_map/ppermute | solution.py:38
  49.9 1.9 %collective-permute-done.18.refs_15_ = bf16[4,256,256]{2,1,0:T(8,128)(2,1)S(1)} collective-permute-done((bf16[4,256,256]{2,1,0:T(8,128)(2,1)S(1)}, bf16[4,256,256]{2,1,0:T(8,128)(2,1)S(1)}, u32[]{:S(2)}, u32[]{:S(2)}) %collective-permute-start.18) | collective-permute-done | bytes 524320 | tf_op jit(solution)/shard_map/ppermute | solution.py:49
  52.6 2.1 %collective-permute-start.23 = (bf16[1024,256]{1,0:T(8,128)(2,1)S(1)}, bf16[1024,256]{1,0:T(8,128)(2,1)S(1)}, u32[]{:S(2)}, u32[]{:S(2)}) collective-permute-start(bf16[1024,256]{1,0:T(8,128)(2,1)S(1)} %products.5), channel_id=1, source_target_pairs={{0,4},{1,5},{2,6},{3,7},{4,8},{5,9},{6,10},{7,11},{8,12},{9,13},{1... | collective-permute-start | bytes 1572872 | tf_op jit(solution)/shard_map/ppermute | solution.py:45
  54.6 1.3 %products.3 = (bf16[1024,256]{1,0:T(8,128)(2,1)S(1)}, bf16[1024,256]{1,0:T(8,128)(2,1)S(1)}) custom-call(bf16[1024,256]{1,0:T(8,128)(2,1)S(1)} %get-tuple-element.18.refs_0_, bf16[1024,256]{1,0:T(8,128)(2,1)S(1)} %collective-permute-done.2.refs_1_, bf16[1024,256]{1,0:T(8,128)(2,1)S(1)} %collective-permute-done.5.refs_2_, ...), custom_call_target="tpu_custom_call" | custom-call | tf_op jit(solution)/shard_map/products/pallas_call | solution.py:192
  56.0 1.9 %collective-permute-start.19 = (bf16[1024,256]{1,0:T(8,128)(2,1)S(1)}, bf16[1024,256]{1,0:T(8,128)(2,1)S(1)}, u32[]{:S(2)}, u32[]{:S(2)}) collective-permute-start(bf16[1024,256]{1,0:T(8,128)(2,1)S(1)} %get-tuple-element.26), channel_id=1, source_target_pairs={{0,4},{1,5},{2,6},{3,7},{4,8},{5,9},{6,10},{7,11},{8,12},{9,13},{1... | collective-permute-start | bytes 1572872 | tf_op jit(solution)/shard_map/ppermute | solution.py:45
  57.9 4.7 %products.4 = (bf16[1024,256]{1,0:T(8,128)(2,1)S(1)}, bf16[1024,256]{1,0:T(8,128)(2,1)S(1)}, bf16[1024,256]{1,0:T(8,128)(2,1)S(1)}, bf16[1024,256]{1,0:T(8,128)(2,1)S(1)}, f32[1024,256]{1,0:T(8,128)S(1)}) custom-call(bf16[1024,256]{1,0:T(8,128)(2,1)S(1)} %get-tuple-element.18.refs_0_, bf16[1024,256]{1,0:T(8,128)(2,1)S(1)} %collective-permute-done.2.refs_1_, ...), custom_call_target="tpu_custom_call" | custom-call | tf_op jit(solution)/shard_map/products/pallas_call | solution.py:192
  62.6 3.1 %collective-permute-done.23 = bf16[1024,256]{1,0:T(8,128)(2,1)S(1)} collective-permute-done((bf16[1024,256]{1,0:T(8,128)(2,1)S(1)}, bf16[1024,256]{1,0:T(8,128)(2,1)S(1)}, u32[]{:S(2)}, u32[]{:S(2)}) %collective-permute-start.23) | collective-permute-done | bytes 524320 | tf_op jit(solution)/shard_map/ppermute | solution.py:45
  66.0 5.4 %collective-permute-done.19 = bf16[1024,256]{1,0:T(8,128)(2,1)S(1)} collective-permute-done((bf16[1024,256]{1,0:T(8,128)(2,1)S(1)}, bf16[1024,256]{1,0:T(8,128)(2,1)S(1)}, u32[]{:S(2)}, u32[]{:S(2)}) %collective-permute-start.19) | collective-permute-done | bytes 524320 | tf_op jit(solution)/shard_map/ppermute | solution.py:45
  71.6 5.4 %collective-permute-done.24 = bf16[1024,256]{1,0:T(8,128)(2,1)S(1)} collective-permute-done((bf16[1024,256]{1,0:T(8,128)(2,1)S(1)}, bf16[1024,256]{1,0:T(8,128)(2,1)S(1)}, u32[]{:S(2)}, u32[]{:S(2)}) %collective-permute-start.24) | collective-permute-done | bytes 524320 | tf_op jit(solution)/shard_map/ppermute | solution.py:45
  77.2 5.4 %collective-permute-done.20 = bf16[1024,256]{1,0:T(8,128)(2,1)S(1)} collective-permute-done((bf16[1024,256]{1,0:T(8,128)(2,1)S(1)}, bf16[1024,256]{1,0:T(8,128)(2,1)S(1)}, u32[]{:S(2)}, u32[]{:S(2)}) %collective-permute-start.20) | collective-permute-done | bytes 524320 | tf_op jit(solution)/shard_map/ppermute | solution.py:45
  82.8 5.4 %collective-permute-done.25 = bf16[1024,256]{1,0:T(8,128)(2,1)S(1)} collective-permute-done((bf16[1024,256]{1,0:T(8,128)(2,1)S(1)}, bf16[1024,256]{1,0:T(8,128)(2,1)S(1)}, u32[]{:S(2)}, u32[]{:S(2)}) %collective-permute-start.25) | collective-permute-done | bytes 524320 | tf_op jit(solution)/shard_map/ppermute | solution.py:45
  88.4 5.5 %collective-permute-done.21 = bf16[1024,256]{1,0:T(8,128)(2,1)} collective-permute-done((bf16[1024,256]{1,0:T(8,128)(2,1)S(1)}, bf16[1024,256]{1,0:T(8,128)(2,1)}, u32[]{:S(2)}, u32[]{:S(2)}) %collective-permute-start.21) | collective-permute-done | bytes 524320 | tf_op jit(solution)/shard_map/ppermute | solution.py:45
  94.6 1.6 %collective-permute-done.1 = bf16[128,1024]{1,0:T(8,128)(2,1)S(1)} collective-permute-done((bf16[128,1024]{1,0:T(8,128)(2,1)S(1)}, bf16[128,1024]{1,0:T(8,128)(2,1)S(1)}, u32[]{:S(2)}, u32[]{:S(2)}) %collective-permute-start.1) | collective-permute-done | bytes 262176 | tf_op jit(solution)/shard_map/ppermute | solution.py:49
  97.1 2.3 %collective-permute-done.26 = bf16[1024,256]{1,0:T(8,128)(2,1)S(1)} collective-permute-done((bf16[1024,256]{1,0:T(8,128)(2,1)S(1)}, bf16[1024,256]{1,0:T(8,128)(2,1)S(1)}, u32[]{:S(2)}, u32[]{:S(2)}) %collective-permute-start.26) | collective-permute-done | bytes 524320 | tf_op jit(solution)/shard_map/ppermute | solution.py:45
  99.5 1.1 %convert_add_fusion = f32[1024,256]{1,0:T(8,128)} fusion(bf16[1024,256]{1,0:T(8,128)(2,1)S(1)} %collective-permute-done.26, f32[1024,256]{1,0:T(8,128)S(1)} %get-tuple-element.25, bf16[1024,256]{1,0:T(8,128)(2,1)S(1)} %collective-permute-done.22), kind=kLoop, calls=%fused_computation | loop fusion | flops 1048576 | bytes 3145728 | tf_op jit(solution)/shard_map/add | solution.py:239
  (42 shorter events, 6.4 us)
Async XLA Ops:
  3.8 4.1 %collective-permute-start = (bf16[56,128,128]{2,1,0:T(8,128)(2,1)}, bf16[56,128,128]{2,1,0:T(8,128)(2,1)S(1)}, u32[]{:S(2)}, u32[]{:S(2)}) collective-permute-start(bf16[56,128,128]{2,1,0:T(8,128)(2,1)} %pack_away.1), channel_id=1, source_target_pairs={{0,128},{128,0},{1,129},{129,1},{2,130},{130,2},{3,131},{131,3},{4... | collective-permute-start | bytes 5505032 | tf_op jit(solution)/shard_map/ppermute | solution.py:49
  4.0 3.9 %copy-start.1 = (s32[1,2,16]{2,1,0:T(2,128)S(1)}, s32[1,2,16]{2,1,0:T(2,128)}, u32[]{:S(2)}) copy-start(s32[1,2,16]{2,1,0:T(2,128)} %param.7) | copy-start | bytes 388
  7.9 1.5 %copy-start = (bf16[56,128,128]{2,1,0:T(8,128)(2,1)S(1)}, bf16[56,128,128]{2,1,0:T(8,128)(2,1)}, u32[]{:S(2)}) copy-start(bf16[56,128,128]{2,1,0:T(8,128)(2,1)} %pack_here.1.kept) | copy-start | bytes 5505028
  16.7 7.9 %collective-permute-start.11 = (bf16[256,256]{1,0:T(8,128)(2,1)S(1)}, bf16[256,256]{1,0:T(8,128)(2,1)S(1)}, u32[]{:S(2)}, u32[]{:S(2)}) collective-permute-start(bf16[256,256]{1,0:T(8,128)(2,1)S(1)} %get-tuple-element.33), channel_id=1, source_target_pairs={{0,2},{1,3},{2,0},{3,1},{4,6},{5,7},{6,4},{7,5},{8,10},{9,11},{10,... | collective-permute-start | bytes 393224 | tf_op jit(solution)/shard_map/ppermute | solution.py:30
  19.2 7.5 %collective-permute-start.10 = (bf16[256,256]{1,0:T(8,128)(2,1)S(1)}, bf16[256,256]{1,0:T(8,128)(2,1)S(1)}, u32[]{:S(2)}, u32[]{:S(2)}) collective-permute-start(bf16[256,256]{1,0:T(8,128)(2,1)S(1)} %get-tuple-element.34), channel_id=1, source_target_pairs={{0,3},{1,0},{2,1},{3,2},{4,7},{5,4},{6,5},{7,6},{8,11},{9,8},{10,9... | collective-permute-start | bytes 393224 | tf_op jit(solution)/shard_map/ppermute | solution.py:30
  20.4 6.3 %collective-permute-start.9 = (bf16[256,256]{1,0:T(8,128)(2,1)S(1)}, bf16[256,256]{1,0:T(8,128)(2,1)S(1)}, u32[]{:S(2)}, u32[]{:S(2)}) collective-permute-start(bf16[256,256]{1,0:T(8,128)(2,1)S(1)} %get-tuple-element.35), channel_id=1, source_target_pairs={{0,1},{1,2},{2,3},{3,0},{4,5},{5,6},{6,7},{7,4},{8,9},{9,10},{10,1... | collective-permute-start | bytes 393224 | tf_op jit(solution)/shard_map/ppermute | solution.py:30
  21.2 7.5 %collective-permute-start.3 = (bf16[1024,256]{1,0:T(8,128)(2,1)S(1)}, bf16[1024,256]{1,0:T(8,128)(2,1)S(1)}, u32[]{:S(2)}, u32[]{:S(2)}) collective-permute-start(bf16[1024,256]{1,0:T(8,128)(2,1)S(1)} %get-tuple-element.18.refs_0_), channel_id=1, source_target_pairs={{0,128},{128,0},{1,129},{129,1},{2,130},{130,2},{3,131},{131,3},{4... | collective-permute-start | bytes 1572872 | tf_op jit(solution)/shard_map/ppermute | solution.py:49
  21.2 11.1 %collective-permute-start.2 = (bf16[1024,256]{1,0:T(8,128)(2,1)S(1)}, bf16[1024,256]{1,0:T(8,128)(2,1)S(1)}, u32[]{:S(2)}, u32[]{:S(2)}) collective-permute-start(bf16[1024,256]{1,0:T(8,128)(2,1)S(1)} %get-tuple-element.18.refs_0_), channel_id=1, source_target_pairs={{0,1},{1,2},{2,3},{3,0},{4,5},{5,6},{6,7},{7,4},{8,9},{9,10},{10,1... | collective-permute-start | bytes 1572872 | tf_op jit(solution)/shard_map/ppermute | solution.py:45
  26.8 7.0 %collective-permute-start.13 = (bf16[4,256,256]{2,1,0:T(8,128)(2,1)S(1)}, bf16[4,256,256]{2,1,0:T(8,128)(2,1)S(1)}, u32[]{:S(2)}, u32[]{:S(2)}) collective-permute-start(bf16[4,256,256]{2,1,0:T(8,128)(2,1)S(1)} %pad_maximum_fusion.refs_8_), channel_id=1, source_target_pairs={{0,128},{128,0},{1,129},{129,1},{2,130},{130,2},{3,131},{131,3},{4... | collective-permute-start | bytes 1572872 | tf_op jit(solution)/shard_map/ppermute | solution.py:49
  27.1 10.5 %collective-permute-start.12 = (bf16[4,256,256]{2,1,0:T(8,128)(2,1)S(1)}, bf16[4,256,256]{2,1,0:T(8,128)(2,1)S(1)}, u32[]{:S(2)}, u32[]{:S(2)}) collective-permute-start(bf16[4,256,256]{2,1,0:T(8,128)(2,1)S(1)} %pad_maximum_fusion.refs_8_), channel_id=1, source_target_pairs={{0,32},{32,64},{64,96},{96,0},{128,224},{160,128},{192,160},{224,1... | collective-permute-start | bytes 1572872 | tf_op jit(solution)/shard_map/ppermute | solution.py:38
  28.7 9.3 %collective-permute-start.4 = (bf16[1024,256]{1,0:T(8,128)(2,1)S(1)}, bf16[1024,256]{1,0:T(8,128)(2,1)S(1)}, u32[]{:S(2)}, u32[]{:S(2)}) collective-permute-start(bf16[1024,256]{1,0:T(8,128)(2,1)S(1)} %collective-permute-done.3.refs_4_), channel_id=1, source_target_pairs={{0,1},{1,2},{2,3},{3,0},{4,5},{5,6},{6,7},{7,4},{8,9},{9,10},{10,1... | collective-permute-start | bytes 1572872 | tf_op jit(solution)/shard_map/ppermute | solution.py:45
  32.4 6.9 %collective-permute-start.7 = (bf16[1024,256]{1,0:T(8,128)(2,1)S(1)}, bf16[1024,256]{1,0:T(8,128)(2,1)S(1)}, u32[]{:S(2)}, u32[]{:S(2)}) collective-permute-start(bf16[1024,256]{1,0:T(8,128)(2,1)S(1)} %collective-permute-done.2.refs_1_), channel_id=1, source_target_pairs={{0,128},{128,0},{1,129},{129,1},{2,130},{130,2},{3,131},{131,3},{4... | collective-permute-start | bytes 1572872 | tf_op jit(solution)/shard_map/ppermute | solution.py:49
  32.4 11.2 %collective-permute-start.6 = (bf16[1024,256]{1,0:T(8,128)(2,1)S(1)}, bf16[1024,256]{1,0:T(8,128)(2,1)S(1)}, u32[]{:S(2)}, u32[]{:S(2)}) collective-permute-start(bf16[1024,256]{1,0:T(8,128)(2,1)S(1)} %collective-permute-done.2.refs_1_), channel_id=1, source_target_pairs={{0,1},{1,2},{2,3},{3,0},{4,5},{5,6},{6,7},{7,4},{8,9},{9,10},{10,1... | collective-permute-start | bytes 1572872 | tf_op jit(solution)/shard_map/ppermute | solution.py:45
  33.9 10.4 %collective-permute-start.14 = (bf16[4,256,256]{2,1,0:T(8,128)(2,1)S(1)}, bf16[4,256,256]{2,1,0:T(8,128)(2,1)S(1)}, u32[]{:S(2)}, u32[]{:S(2)}) collective-permute-start(bf16[4,256,256]{2,1,0:T(8,128)(2,1)S(1)} %collective-permute-done.13.refs_12_), channel_id=1, source_target_pairs={{0,32},{32,64},{64,96},{96,0},{128,224},{160,128},{192,160},{224,1... | collective-permute-start | bytes 1572872 | tf_op jit(solution)/shard_map/ppermute | solution.py:38
  37.6 12.3 %collective-permute-start.16 = (bf16[4,256,256]{2,1,0:T(8,128)(2,1)S(1)}, bf16[4,256,256]{2,1,0:T(8,128)(2,1)S(1)}, u32[]{:S(2)}, u32[]{:S(2)}) collective-permute-start(bf16[4,256,256]{2,1,0:T(8,128)(2,1)S(1)} %collective-permute-done.12.refs_9_), channel_id=1, source_target_pairs={{0,32},{32,64},{64,96},{96,0},{128,224},{160,128},{192,160},{224,1... | collective-permute-start | bytes 1572872 | tf_op jit(solution)/shard_map/ppermute | solution.py:38
  38.0 11.9 %collective-permute-start.17 = (bf16[4,256,256]{2,1,0:T(8,128)(2,1)S(1)}, bf16[4,256,256]{2,1,0:T(8,128)(2,1)S(1)}, u32[]{:S(2)}, u32[]{:S(2)}) collective-permute-start(bf16[4,256,256]{2,1,0:T(8,128)(2,1)S(1)} %collective-permute-done.12.refs_9_), channel_id=1, source_target_pairs={{0,128},{128,0},{1,129},{129,1},{2,130},{130,2},{3,131},{131,3},{4... | collective-permute-start | bytes 1572872 | tf_op jit(solution)/shard_map/ppermute | solution.py:49
  39.3 10.5 %collective-permute-start.5 = (bf16[1024,256]{1,0:T(8,128)(2,1)S(1)}, bf16[1024,256]{1,0:T(8,128)(2,1)S(1)}, u32[]{:S(2)}, u32[]{:S(2)}) collective-permute-start(bf16[1024,256]{1,0:T(8,128)(2,1)S(1)} %collective-permute-done.4.refs_5_), channel_id=1, source_target_pairs={{0,128},{128,0},{1,129},{129,1},{2,130},{130,2},{3,131},{131,3},{4... | collective-permute-start | bytes 1572872 | tf_op jit(solution)/shard_map/ppermute | solution.py:49
  43.6 6.3 %collective-permute-start.8 = (bf16[1024,256]{1,0:T(8,128)(2,1)S(1)}, bf16[1024,256]{1,0:T(8,128)(2,1)S(1)}, u32[]{:S(2)}, u32[]{:S(2)}) collective-permute-start(bf16[1024,256]{1,0:T(8,128)(2,1)S(1)} %collective-permute-done.6.refs_3_), channel_id=1, source_target_pairs={{0,128},{128,0},{1,129},{129,1},{2,130},{130,2},{3,131},{131,3},{4... | collective-permute-start | bytes 1572872 | tf_op jit(solution)/shard_map/ppermute | solution.py:49
  44.2 5.6 %collective-permute-start.15 = (bf16[4,256,256]{2,1,0:T(8,128)(2,1)S(1)}, bf16[4,256,256]{2,1,0:T(8,128)(2,1)S(1)}, u32[]{:S(2)}, u32[]{:S(2)}) collective-permute-start(bf16[4,256,256]{2,1,0:T(8,128)(2,1)S(1)} %collective-permute-done.14.refs_13_), channel_id=1, source_target_pairs={{0,128},{128,0},{1,129},{129,1},{2,130},{130,2},{3,131},{131,3},{4... | collective-permute-start | bytes 1572872 | tf_op jit(solution)/shard_map/ppermute | solution.py:49
  49.9 1.9 %collective-permute-start.18 = (bf16[4,256,256]{2,1,0:T(8,128)(2,1)S(1)}, bf16[4,256,256]{2,1,0:T(8,128)(2,1)S(1)}, u32[]{:S(2)}, u32[]{:S(2)}) collective-permute-start(bf16[4,256,256]{2,1,0:T(8,128)(2,1)S(1)} %collective-permute-done.16.refs_11_), channel_id=1, source_target_pairs={{0,128},{128,0},{1,129},{129,1},{2,130},{130,2},{3,131},{131,3},{4... | collective-permute-start | bytes 1572872 | tf_op jit(solution)/shard_map/ppermute | solution.py:49
  52.6 13.2 %collective-permute-start.23 = (bf16[1024,256]{1,0:T(8,128)(2,1)S(1)}, bf16[1024,256]{1,0:T(8,128)(2,1)S(1)}, u32[]{:S(2)}, u32[]{:S(2)}) collective-permute-start(bf16[1024,256]{1,0:T(8,128)(2,1)S(1)} %products.5), channel_id=1, source_target_pairs={{0,4},{1,5},{2,6},{3,7},{4,8},{5,9},{6,10},{7,11},{8,12},{9,13},{1... | collective-permute-start | bytes 1572872 | tf_op jit(solution)/shard_map/ppermute | solution.py:45
  56.0 15.4 %collective-permute-start.19 = (bf16[1024,256]{1,0:T(8,128)(2,1)S(1)}, bf16[1024,256]{1,0:T(8,128)(2,1)S(1)}, u32[]{:S(2)}, u32[]{:S(2)}) collective-permute-start(bf16[1024,256]{1,0:T(8,128)(2,1)S(1)} %get-tuple-element.26), channel_id=1, source_target_pairs={{0,4},{1,5},{2,6},{3,7},{4,8},{5,9},{6,10},{7,11},{8,12},{9,13},{1... | collective-permute-start | bytes 1572872 | tf_op jit(solution)/shard_map/ppermute | solution.py:45
  65.9 11.1 %collective-permute-start.24 = (bf16[1024,256]{1,0:T(8,128)(2,1)S(1)}, bf16[1024,256]{1,0:T(8,128)(2,1)S(1)}, u32[]{:S(2)}, u32[]{:S(2)}) collective-permute-start(bf16[1024,256]{1,0:T(8,128)(2,1)S(1)} %add_convert_fusion.2), channel_id=1, source_target_pairs={{0,4},{1,5},{2,6},{3,7},{4,8},{5,9},{6,10},{7,11},{8,12},{9,13},{1... | collective-permute-start | bytes 1572872 | tf_op jit(solution)/shard_map/ppermute | solution.py:45
  71.5 11.1 %collective-permute-start.20 = (bf16[1024,256]{1,0:T(8,128)(2,1)S(1)}, bf16[1024,256]{1,0:T(8,128)(2,1)S(1)}, u32[]{:S(2)}, u32[]{:S(2)}) collective-permute-start(bf16[1024,256]{1,0:T(8,128)(2,1)S(1)} %add_convert_fusion.4), channel_id=1, source_target_pairs={{0,4},{1,5},{2,6},{3,7},{4,8},{5,9},{6,10},{7,11},{8,12},{9,13},{1... | collective-permute-start | bytes 1572872 | tf_op jit(solution)/shard_map/ppermute | solution.py:45
  77.1 11.1 %collective-permute-start.25 = (bf16[1024,256]{1,0:T(8,128)(2,1)S(1)}, bf16[1024,256]{1,0:T(8,128)(2,1)S(1)}, u32[]{:S(2)}, u32[]{:S(2)}) collective-permute-start(bf16[1024,256]{1,0:T(8,128)(2,1)S(1)} %add_convert_fusion.1), channel_id=1, source_target_pairs={{0,4},{1,5},{2,6},{3,7},{4,8},{5,9},{6,10},{7,11},{8,12},{9,13},{1... | collective-permute-start | bytes 1572872 | tf_op jit(solution)/shard_map/ppermute | solution.py:45
  82.7 11.2 %collective-permute-start.21 = (bf16[1024,256]{1,0:T(8,128)(2,1)S(1)}, bf16[1024,256]{1,0:T(8,128)(2,1)}, u32[]{:S(2)}, u32[]{:S(2)}) collective-permute-start(bf16[1024,256]{1,0:T(8,128)(2,1)S(1)} %add_convert_fusion.3), channel_id=1, source_target_pairs={{0,4},{1,5},{2,6},{3,7},{4,8},{5,9},{6,10},{7,11},{8,12},{9,13},{1... | collective-permute-start | bytes 1572872 | tf_op jit(solution)/shard_map/ppermute | solution.py:45
  88.4 11.1 %collective-permute-start.26 = (bf16[1024,256]{1,0:T(8,128)(2,1)S(1)}, bf16[1024,256]{1,0:T(8,128)(2,1)S(1)}, u32[]{:S(2)}, u32[]{:S(2)}) collective-permute-start(bf16[1024,256]{1,0:T(8,128)(2,1)S(1)} %add_convert_fusion), channel_id=1, source_target_pairs={{0,4},{1,5},{2,6},{3,7},{4,8},{5,9},{6,10},{7,11},{8,12},{9,13},{1... | collective-permute-start | bytes 1572872 | tf_op jit(solution)/shard_map/ppermute | solution.py:45
  93.9 5.5 %collective-permute-start.22 = (bf16[1024,256]{1,0:T(8,128)(2,1)}, bf16[1024,256]{1,0:T(8,128)(2,1)S(1)}, u32[]{:S(2)}, u32[]{:S(2)}) collective-permute-start(bf16[1024,256]{1,0:T(8,128)(2,1)} %collective-permute-done.21), channel_id=1, source_target_pairs={{0,128},{128,0},{1,129},{129,1},{2,130},{130,2},{3,131},{131,3},{4... | collective-permute-start | bytes 1572872 | tf_op jit(solution)/shard_map/ppermute | solution.py:49
  94.0 2.2 %collective-permute-start.1 = (bf16[128,1024]{1,0:T(8,128)(2,1)S(1)}, bf16[128,1024]{1,0:T(8,128)(2,1)S(1)}, u32[]{:S(2)}, u32[]{:S(2)}) collective-permute-start(bf16[128,1024]{1,0:T(8,128)(2,1)S(1)} %get-tuple-element.37), channel_id=1, source_target_pairs={{0,128},{128,0},{1,129},{129,1},{2,130},{130,2},{3,131},{131,3},{4... | collective-permute-start | bytes 786440 | tf_op jit(solution)/shard_map/ppermute | solution.py:49

commit v3 on v1

--- a/solution.py
+++ b/solution.py
@@ -218,7 +218,8 @@
 
     mine = jnp.stack([share(0), hop(share(1), 1), hop(share(-1), -1), hop(share(2), 2)])
     x1 = toward(mine, "x")
-    y1 = toward(turned, "y")
+    whole, _ = lax.optimization_barrier((turned, mine))
+    y1 = toward(whole, "y")
     mine_other, turned_other = swap(mine), swap(turned)
     x1_other, y1_other = toward(mine_other, "x"), toward(turned_other, "y")
     x2, y2 = toward(x1, "x"), toward(y1, "y")

time: 101 us -> 105 us (1.040)
  waiting for transfers between devices: 55 us -> 59.6 us
    ppermute x10, waiting for transfers between devices: 38.7 us -> 43.7 us  [toward(): return lax.ppermute(value, ('ctx', 'doc'), pairs)]
    ppermute x3, waiting for transfers between devices: 8.05 us -> 6.24 us  [toward(): return lax.ppermute(value, ('ctx', 'head'), pairs)]
    ppermute x11, starting transfers between devices: 2.93 us -> 1.21 us  [swap(): return lax.ppermute(value, 'ctx', [(0, 1), (1, 0)])]
    ppermute x3, waiting for transfers between devices: 4.32 us -> 5.72 us  [hop(): return lax.ppermute(value, 'doc', pairs)]
    ppermute x3, starting transfers between devices: 3.35 us -> 4.44 us  [toward(): return lax.ppermute(value, ('ctx', 'head'), pairs)]
  transfers between devices with their start and end apart: 27 -> 27, of which waited for: 18 -> 18; matrix products, arithmetic and copies ran while one was open for 2% -> 2% of each run, Pallas kernels for 10% -> 9%
where the time goes in v3:
time: 105 us; the launch traced here: 104 us
  waiting for transfers between devices  59.6 us (57%)
  Pallas kernels  20.8 us (20%)
  starting transfers between devices  18.6 us (18%)
  other arithmetic  2.75 us (3%)
  local copies, waits for them, and re-layouts  1.59 us (2%)
    ppermute x10, waiting for transfers between devices, toward(): return lax.ppermute(value, ('ctx', 'doc'), pairs)  43.7 us
    ppermute x10, starting transfers between devices, toward(): return lax.ppermute(value, ('ctx', 'doc'), pairs)  8.55 us
    pallas_call x1, Pallas kernels, attend(): pl.pallas_call(attend_kernel, out_shape=(out, jax.ShapeDtypeStruct((width...  7.29 us
    pallas_call x3, Pallas kernels, products(): pl.pallas_call(body, out_shape=[jax.ShapeDtypeStruct((rows, cols), F32 if...  6.89 us
    pallas_call x2, Pallas kernels, pack(): pl.pallas_call(body, out_shape=jax.ShapeDtypeStruct((SENT, BLOCK_TOKENS,...  6.67 us
    ppermute x3, waiting for transfers between devices, toward(): return lax.ppermute(value, ('ctx', 'head'), pairs)  6.24 us
    ppermute x3, waiting for transfers between devices, hop(): return lax.ppermute(value, 'doc', pairs)  5.72 us
    ppermute x3, starting transfers between devices, toward(): return lax.ppermute(value, ('ctx', 'head'), pairs)  4.44 us
  transfers between devices with their start and end apart: 27, of which 18 were waited for; matrix products, arithmetic and copies ran while one was open for 2% of the time, Pallas kernels for 9%

profile of v3, /device:TPU:8, one launch (start us, length us, event | category | flops | bytes accessed | tf_op | source)
XLA Modules:
  0.0 104.3 jit_solution(7152344120594635684)
XLA Ops:
  0.6 3.2 %pack_away.1 = bf16[56,128,128]{2,1,0:T(8,128)(2,1)} custom-call(s32[2,16]{1,0:T(2,128)} %bitcast.12, bf16[128,2048]{1,0:T(8,128)(2,1)} %bitcast.19, bf16[4096,256]{1,0:T(8,128)(2,1)} %bitcast.15, bf16[4096,256]{1,0:T(8,128)(2,1)} %bitcast.17), custom_call_target="tpu_custom_call" | custom-call | tf_op jit(solution)/shard_map/pack_away/pallas_call | solution.py:92
  4.1 3.4 %pack_here.1.kept = bf16[56,128,128]{2,1,0:T(8,128)(2,1)} custom-call(s32[2,16]{1,0:T(2,128)} %bitcast.13, bf16[128,2048]{1,0:T(8,128)(2,1)} %bitcast.20, bf16[4096,256]{1,0:T(8,128)(2,1)} %bitcast.16, bf16[4096,256]{1,0:T(8,128)(2,1)} %bitcast.18), custom_call_target="tpu_custom_call" | custom-call | tf_op jit(solution)/shard_map/pack_here/pallas_call | solution.py:92
  8.0 1.5 %copy-done = bf16[56,128,128]{2,1,0:T(8,128)(2,1)S(1)} copy-done((bf16[56,128,128]{2,1,0:T(8,128)(2,1)S(1)}, bf16[56,128,128]{2,1,0:T(8,128)(2,1)}, u32[]{:S(2)}) %copy-start) | copy-done | bytes 1835032
  9.5 7.3 %attend.1 = (bf16[2,128,1024]{2,1,0:T(8,128)(2,1)S(1)}, bf16[1024,256]{1,0:T(8,128)(2,1)S(1)}) custom-call(s32[2,16]{1,0:T(2,128)S(1)} %bitcast.14, bf16[56,128,128]{2,1,0:T(8,128)(2,1)S(1)} %copy-done, bf16[56,128,128]{2,1,0:T(8,128)(2,1)S(1)} %collective-permute-done.got), custom_call_target="tpu_custom_call" | custom-call | tf_op jit(solution)/shard_map/attend/pallas_call | solution.py:141
  16.8 2.4 %collective-permute-start.4 = (bf16[256,256]{1,0:T(8,128)(2,1)S(1)}, bf16[256,256]{1,0:T(8,128)(2,1)S(1)}, u32[]{:S(2)}, u32[]{:S(2)}) collective-permute-start(bf16[256,256]{1,0:T(8,128)(2,1)S(1)} %get-tuple-element.23), channel_id=1, source_target_pairs={{0,2},{1,3},{2,0},{3,1},{4,6},{5,7},{6,4},{7,5},{8,10},{9,11},{10,... | collective-permute-start | bytes 393224 | tf_op jit(solution)/shard_map/ppermute | solution.py:30
  19.2 1.4 %collective-permute-start.3 = (bf16[256,256]{1,0:T(8,128)(2,1)S(1)}, bf16[256,256]{1,0:T(8,128)(2,1)S(1)}, u32[]{:S(2)}, u32[]{:S(2)}) collective-permute-start(bf16[256,256]{1,0:T(8,128)(2,1)S(1)} %get-tuple-element.24), channel_id=1, source_target_pairs={{0,3},{1,0},{2,1},{3,2},{4,7},{5,4},{6,5},{7,6},{8,11},{9,8},{10,9... | collective-permute-start | bytes 393224 | tf_op jit(solution)/shard_map/ppermute | solution.py:30
  21.2 3.6 %collective-permute-done.4 = bf16[256,256]{1,0:T(8,128)(2,1)S(1)} collective-permute-done((bf16[256,256]{1,0:T(8,128)(2,1)S(1)}, bf16[256,256]{1,0:T(8,128)(2,1)S(1)}, u32[]{:S(2)}, u32[]{:S(2)}) %collective-permute-start.4) | collective-permute-done | bytes 131104 | tf_op jit(solution)/shard_map/ppermute | solution.py:30
  24.8 2.0 %collective-permute-done.3 = bf16[256,256]{1,0:T(8,128)(2,1)S(1)} collective-permute-done((bf16[256,256]{1,0:T(8,128)(2,1)S(1)}, bf16[256,256]{1,0:T(8,128)(2,1)S(1)}, u32[]{:S(2)}, u32[]{:S(2)}) %collective-permute-start.3) | collective-permute-done | bytes 131104 | tf_op jit(solution)/shard_map/ppermute | solution.py:30
  27.0 1.5 %collective-permute-start.5 = (bf16[1024,256]{1,0:T(8,128)(2,1)S(1)}, bf16[1024,256]{1,0:T(8,128)(2,1)S(1)}, u32[]{:S(2)}, u32[]{:S(2)}) collective-permute-start(bf16[1024,256]{1,0:T(8,128)(2,1)S(1)} %get-tuple-element.14.refs_0_), channel_id=1, source_target_pairs={{0,1},{1,2},{2,3},{3,0},{4,5},{5,6},{6,7},{7,4},{8,9},{9,10},{10,1... | collective-permute-start | bytes 1572872 | tf_op jit(solution)/shard_map/ppermute | solution.py:45
  28.5 1.5 %collective-permute-start.12 = (bf16[4,256,256]{2,1,0:T(8,128)(2,1)S(1)}, bf16[4,256,256]{2,1,0:T(8,128)(2,1)S(1)}, u32[]{:S(2)}, u32[]{:S(2)}) collective-permute-start(bf16[4,256,256]{2,1,0:T(8,128)(2,1)S(1)} %pad_maximum_fusion.refs_8_), channel_id=1, source_target_pairs={{0,32},{32,64},{64,96},{96,0},{128,224},{160,128},{192,160},{224,1... | collective-permute-start | bytes 1572872 | tf_op jit(solution)/shard_map/ppermute | solution.py:38
  30.0 1.2 %collective-permute-start.7 = (bf16[1024,256]{1,0:T(8,128)(2,1)S(1)}, bf16[1024,256]{1,0:T(8,128)(2,1)S(1)}, u32[]{:S(2)}, u32[]{:S(2)}) collective-permute-start(bf16[1024,256]{1,0:T(8,128)(2,1)S(1)} %collective-permute-done.6.refs_4_), channel_id=1, source_target_pairs={{0,1},{1,2},{2,3},{3,0},{4,5},{5,6},{6,7},{7,4},{8,9},{9,10},{10,1... | collective-permute-start | bytes 1572872 | tf_op jit(solution)/shard_map/ppermute | solution.py:45
  31.2 5.0 %collective-permute-done.5.refs_1_ = bf16[1024,256]{1,0:T(8,128)(2,1)S(1)} collective-permute-done((bf16[1024,256]{1,0:T(8,128)(2,1)S(1)}, bf16[1024,256]{1,0:T(8,128)(2,1)S(1)}, u32[]{:S(2)}, u32[]{:S(2)}) %collective-permute-start.5) | collective-permute-done | bytes 524320 | tf_op jit(solution)/shard_map/ppermute | solution.py:45
  36.3 1.5 %collective-permute-start.9 = (bf16[1024,256]{1,0:T(8,128)(2,1)S(1)}, bf16[1024,256]{1,0:T(8,128)(2,1)S(1)}, u32[]{:S(2)}, u32[]{:S(2)}) collective-permute-start(bf16[1024,256]{1,0:T(8,128)(2,1)S(1)} %collective-permute-done.5.refs_1_), channel_id=1, source_target_pairs={{0,1},{1,2},{2,3},{3,0},{4,5},{5,6},{6,7},{7,4},{8,9},{9,10},{10,1... | collective-permute-start | bytes 1572872 | tf_op jit(solution)/shard_map/ppermute | solution.py:45
  37.7 1.5 %collective-permute-start.14 = (bf16[4,256,256]{2,1,0:T(8,128)(2,1)S(1)}, bf16[4,256,256]{2,1,0:T(8,128)(2,1)S(1)}, u32[]{:S(2)}, u32[]{:S(2)}) collective-permute-start(bf16[4,256,256]{2,1,0:T(8,128)(2,1)S(1)} %collective-permute-done.13.refs_12_), channel_id=1, source_target_pairs={{0,32},{32,64},{64,96},{96,0},{128,224},{160,128},{192,160},{224,1... | collective-permute-start | bytes 1572872 | tf_op jit(solution)/shard_map/ppermute | solution.py:38
  39.2 1.5 %collective-permute-start.16 = (bf16[4,256,256]{2,1,0:T(8,128)(2,1)S(1)}, bf16[4,256,256]{2,1,0:T(8,128)(2,1)S(1)}, u32[]{:S(2)}, u32[]{:S(2)}) collective-permute-start(bf16[4,256,256]{2,1,0:T(8,128)(2,1)S(1)} %collective-permute-done.12.refs_9_), channel_id=1, source_target_pairs={{0,32},{32,64},{64,96},{96,0},{128,224},{160,128},{192,160},{224,1... | collective-permute-start | bytes 1572872 | tf_op jit(solution)/shard_map/ppermute | solution.py:38
  40.7 1.2 %collective-permute-done.7.refs_5_ = bf16[1024,256]{1,0:T(8,128)(2,1)S(1)} collective-permute-done((bf16[1024,256]{1,0:T(8,128)(2,1)S(1)}, bf16[1024,256]{1,0:T(8,128)(2,1)S(1)}, u32[]{:S(2)}, u32[]{:S(2)}) %collective-permute-start.7) | collective-permute-done | bytes 524320 | tf_op jit(solution)/shard_map/ppermute | solution.py:45
  42.4 5.1 %collective-permute-done.9.refs_3_ = bf16[1024,256]{1,0:T(8,128)(2,1)S(1)} collective-permute-done((bf16[1024,256]{1,0:T(8,128)(2,1)S(1)}, bf16[1024,256]{1,0:T(8,128)(2,1)S(1)}, u32[]{:S(2)}, u32[]{:S(2)}) %collective-permute-start.9) | collective-permute-done | bytes 524320 | tf_op jit(solution)/shard_map/ppermute | solution.py:45
  48.1 5.6 %collective-permute-done.16.refs_11_ = bf16[4,256,256]{2,1,0:T(8,128)(2,1)S(1)} collective-permute-done((bf16[4,256,256]{2,1,0:T(8,128)(2,1)S(1)}, bf16[4,256,256]{2,1,0:T(8,128)(2,1)S(1)}, u32[]{:S(2)}, u32[]{:S(2)}) %collective-permute-start.16) | collective-permute-done | bytes 524320 | tf_op jit(solution)/shard_map/ppermute | solution.py:38
  53.8 1.9 %collective-permute-done.18.refs_15_ = bf16[4,256,256]{2,1,0:T(8,128)(2,1)S(1)} collective-permute-done((bf16[4,256,256]{2,1,0:T(8,128)(2,1)S(1)}, bf16[4,256,256]{2,1,0:T(8,128)(2,1)S(1)}, u32[]{:S(2)}, u32[]{:S(2)}) %collective-permute-start.18) | collective-permute-done | bytes 524320 | tf_op jit(solution)/shard_map/ppermute | solution.py:49
  56.4 1.9 %collective-permute-start.23 = (bf16[1024,256]{1,0:T(8,128)(2,1)S(1)}, bf16[1024,256]{1,0:T(8,128)(2,1)S(1)}, u32[]{:S(2)}, u32[]{:S(2)}) collective-permute-start(bf16[1024,256]{1,0:T(8,128)(2,1)S(1)} %products.5), channel_id=1, source_target_pairs={{0,4},{1,5},{2,6},{3,7},{4,8},{5,9},{6,10},{7,11},{8,12},{9,13},{1... | collective-permute-start | bytes 1572872 | tf_op jit(solution)/shard_map/ppermute | solution.py:45
  58.3 1.3 %products.4 = (bf16[1024,256]{1,0:T(8,128)(2,1)S(1)}, bf16[1024,256]{1,0:T(8,128)(2,1)S(1)}) custom-call(bf16[1024,256]{1,0:T(8,128)(2,1)S(1)} %get-tuple-element.14.refs_0_, bf16[1024,256]{1,0:T(8,128)(2,1)S(1)} %collective-permute-done.5.refs_1_, bf16[1024,256]{1,0:T(8,128)(2,1)S(1)} %collective-permute-done.8.refs_2_, ...), custom_call_target="tpu_custom_call" | custom-call | tf_op jit(solution)/shard_map/products/pallas_call | solution.py:192
  59.7 2.0 %collective-permute-start.19 = (bf16[1024,256]{1,0:T(8,128)(2,1)S(1)}, bf16[1024,256]{1,0:T(8,128)(2,1)S(1)}, u32[]{:S(2)}, u32[]{:S(2)}) collective-permute-start(bf16[1024,256]{1,0:T(8,128)(2,1)S(1)} %get-tuple-element.16), channel_id=1, source_target_pairs={{0,4},{1,5},{2,6},{3,7},{4,8},{5,9},{6,10},{7,11},{8,12},{9,13},{1... | collective-permute-start | bytes 1572872 | tf_op jit(solution)/shard_map/ppermute | solution.py:45
  61.7 7.8 %collective-permute-done.23 = bf16[1024,256]{1,0:T(8,128)(2,1)S(1)} collective-permute-done((bf16[1024,256]{1,0:T(8,128)(2,1)S(1)}, bf16[1024,256]{1,0:T(8,128)(2,1)S(1)}, u32[]{:S(2)}, u32[]{:S(2)}) %collective-permute-start.23) | collective-permute-done | bytes 524320 | tf_op jit(solution)/shard_map/ppermute | solution.py:45
  69.7 4.8 %products.3 = (bf16[1024,256]{1,0:T(8,128)(2,1)S(1)}, bf16[1024,256]{1,0:T(8,128)(2,1)S(1)}, bf16[1024,256]{1,0:T(8,128)(2,1)S(1)}, bf16[1024,256]{1,0:T(8,128)(2,1)S(1)}, f32[1024,256]{1,0:T(8,128)S(1)}) custom-call(bf16[1024,256]{1,0:T(8,128)(2,1)S(1)} %get-tuple-element.14.refs_0_, bf16[1024,256]{1,0:T(8,128)(2,1)S(1)} %collective-permute-done.5.refs_1_, ...), custom_call_target="tpu_custom_call" | custom-call | tf_op jit(solution)/shard_map/products/pallas_call | solution.py:192
  75.3 5.4 %collective-permute-done.24 = bf16[1024,256]{1,0:T(8,128)(2,1)S(1)} collective-permute-done((bf16[1024,256]{1,0:T(8,128)(2,1)S(1)}, bf16[1024,256]{1,0:T(8,128)(2,1)S(1)}, u32[]{:S(2)}, u32[]{:S(2)}) %collective-permute-start.24) | collective-permute-done | bytes 524320 | tf_op jit(solution)/shard_map/ppermute | solution.py:45
  80.9 5.4 %collective-permute-done.20 = bf16[1024,256]{1,0:T(8,128)(2,1)S(1)} collective-permute-done((bf16[1024,256]{1,0:T(8,128)(2,1)S(1)}, bf16[1024,256]{1,0:T(8,128)(2,1)S(1)}, u32[]{:S(2)}, u32[]{:S(2)}) %collective-permute-start.20) | collective-permute-done | bytes 524320 | tf_op jit(solution)/shard_map/ppermute | solution.py:45
  86.5 5.4 %collective-permute-done.25 = bf16[1024,256]{1,0:T(8,128)(2,1)S(1)} collective-permute-done((bf16[1024,256]{1,0:T(8,128)(2,1)S(1)}, bf16[1024,256]{1,0:T(8,128)(2,1)S(1)}, u32[]{:S(2)}, u32[]{:S(2)}) %collective-permute-start.25) | collective-permute-done | bytes 524320 | tf_op jit(solution)/shard_map/ppermute | solution.py:45
  92.1 5.5 %collective-permute-done.21 = bf16[1024,256]{1,0:T(8,128)(2,1)} collective-permute-done((bf16[1024,256]{1,0:T(8,128)(2,1)S(1)}, bf16[1024,256]{1,0:T(8,128)(2,1)}, u32[]{:S(2)}, u32[]{:S(2)}) %collective-permute-start.21) | collective-permute-done | bytes 524320 | tf_op jit(solution)/shard_map/ppermute | solution.py:45
  98.3 1.6 %collective-permute-done.1 = bf16[128,1024]{1,0:T(8,128)(2,1)S(1)} collective-permute-done((bf16[128,1024]{1,0:T(8,128)(2,1)S(1)}, bf16[128,1024]{1,0:T(8,128)(2,1)S(1)}, u32[]{:S(2)}, u32[]{:S(2)}) %collective-permute-start.1) | collective-permute-done | bytes 262176 | tf_op jit(solution)/shard_map/ppermute | solution.py:49
  99.9 0.9 maximum_select_fusion
  100.8 2.3 %collective-permute-done.26 = bf16[1024,256]{1,0:T(8,128)(2,1)S(1)} collective-permute-done((bf16[1024,256]{1,0:T(8,128)(2,1)S(1)}, bf16[1024,256]{1,0:T(8,128)(2,1)S(1)}, u32[]{:S(2)}, u32[]{:S(2)}) %collective-permute-start.26) | collective-permute-done | bytes 524320 | tf_op jit(solution)/shard_map/ppermute | solution.py:45
  103.2 1.1 %convert_add_fusion = f32[1024,256]{1,0:T(8,128)} fusion(bf16[1024,256]{1,0:T(8,128)(2,1)S(1)} %collective-permute-done.26, f32[1024,256]{1,0:T(8,128)S(1)} %get-tuple-element.15, bf16[1024,256]{1,0:T(8,128)(2,1)S(1)} %collective-permute-done.22), kind=kLoop, calls=%fused_computation | loop fusion | flops 1048576 | bytes 3145728 | tf_op jit(solution)/shard_map/add | solution.py:239
  (42 shorter events, 5.7 us)
Async XLA Ops:
  3.9 4.1 %collective-permute-start = (bf16[56,128,128]{2,1,0:T(8,128)(2,1)}, bf16[56,128,128]{2,1,0:T(8,128)(2,1)S(1)}, u32[]{:S(2)}, u32[]{:S(2)}) collective-permute-start(bf16[56,128,128]{2,1,0:T(8,128)(2,1)} %pack_away.1), channel_id=1, source_target_pairs={{0,128},{128,0},{1,129},{129,1},{2,130},{130,2},{3,131},{131,3},{4... | collective-permute-start | bytes 5505032 | tf_op jit(solution)/shard_map/ppermute | solution.py:49
  4.1 3.9 %copy-start.1 = (s32[1,2,16]{2,1,0:T(2,128)S(1)}, s32[1,2,16]{2,1,0:T(2,128)}, u32[]{:S(2)}) copy-start(s32[1,2,16]{2,1,0:T(2,128)} %param.7) | copy-start | bytes 388
  8.0 1.5 %copy-start = (bf16[56,128,128]{2,1,0:T(8,128)(2,1)S(1)}, bf16[56,128,128]{2,1,0:T(8,128)(2,1)}, u32[]{:S(2)}) copy-start(bf16[56,128,128]{2,1,0:T(8,128)(2,1)} %pack_here.1.kept) | copy-start | bytes 5505028
  16.8 7.9 %collective-permute-start.4 = (bf16[256,256]{1,0:T(8,128)(2,1)S(1)}, bf16[256,256]{1,0:T(8,128)(2,1)S(1)}, u32[]{:S(2)}, u32[]{:S(2)}) collective-permute-start(bf16[256,256]{1,0:T(8,128)(2,1)S(1)} %get-tuple-element.23), channel_id=1, source_target_pairs={{0,2},{1,3},{2,0},{3,1},{4,6},{5,7},{6,4},{7,5},{8,10},{9,11},{10,... | collective-permute-start | bytes 393224 | tf_op jit(solution)/shard_map/ppermute | solution.py:30
  19.2 7.6 %collective-permute-start.3 = (bf16[256,256]{1,0:T(8,128)(2,1)S(1)}, bf16[256,256]{1,0:T(8,128)(2,1)S(1)}, u32[]{:S(2)}, u32[]{:S(2)}) collective-permute-start(bf16[256,256]{1,0:T(8,128)(2,1)S(1)} %get-tuple-element.24), channel_id=1, source_target_pairs={{0,3},{1,0},{2,1},{3,2},{4,7},{5,4},{6,5},{7,6},{8,11},{9,8},{10,9... | collective-permute-start | bytes 393224 | tf_op jit(solution)/shard_map/ppermute | solution.py:30
  20.6 6.3 %collective-permute-start.2 = (bf16[256,256]{1,0:T(8,128)(2,1)S(1)}, bf16[256,256]{1,0:T(8,128)(2,1)S(1)}, u32[]{:S(2)}, u32[]{:S(2)}) collective-permute-start(bf16[256,256]{1,0:T(8,128)(2,1)S(1)} %get-tuple-element.25), channel_id=1, source_target_pairs={{0,1},{1,2},{2,3},{3,0},{4,5},{5,6},{6,7},{7,4},{8,9},{9,10},{10,1... | collective-permute-start | bytes 393224 | tf_op jit(solution)/shard_map/ppermute | solution.py:30
  21.2 8.8 %collective-permute-start.6 = (bf16[1024,256]{1,0:T(8,128)(2,1)S(1)}, bf16[1024,256]{1,0:T(8,128)(2,1)S(1)}, u32[]{:S(2)}, u32[]{:S(2)}) collective-permute-start(bf16[1024,256]{1,0:T(8,128)(2,1)S(1)} %get-tuple-element.14.refs_0_), channel_id=1, source_target_pairs={{0,128},{128,0},{1,129},{129,1},{2,130},{130,2},{3,131},{131,3},{4... | collective-permute-start | bytes 1572872 | tf_op jit(solution)/shard_map/ppermute | solution.py:49
  27.0 9.3 %collective-permute-start.5 = (bf16[1024,256]{1,0:T(8,128)(2,1)S(1)}, bf16[1024,256]{1,0:T(8,128)(2,1)S(1)}, u32[]{:S(2)}, u32[]{:S(2)}) collective-permute-start(bf16[1024,256]{1,0:T(8,128)(2,1)S(1)} %get-tuple-element.14.refs_0_), channel_id=1, source_target_pairs={{0,1},{1,2},{2,3},{3,0},{4,5},{5,6},{6,7},{7,4},{8,9},{9,10},{10,1... | collective-permute-start | bytes 1572872 | tf_op jit(solution)/shard_map/ppermute | solution.py:45
  28.5 9.2 %collective-permute-start.13 = (bf16[4,256,256]{2,1,0:T(8,128)(2,1)S(1)}, bf16[4,256,256]{2,1,0:T(8,128)(2,1)S(1)}, u32[]{:S(2)}, u32[]{:S(2)}) collective-permute-start(bf16[4,256,256]{2,1,0:T(8,128)(2,1)S(1)} %pad_maximum_fusion.refs_8_), channel_id=1, source_target_pairs={{0,128},{128,0},{1,129},{129,1},{2,130},{130,2},{3,131},{131,3},{4... | collective-permute-start | bytes 1572872 | tf_op jit(solution)/shard_map/ppermute | solution.py:49
  28.5 10.7 %collective-permute-start.12 = (bf16[4,256,256]{2,1,0:T(8,128)(2,1)S(1)}, bf16[4,256,256]{2,1,0:T(8,128)(2,1)S(1)}, u32[]{:S(2)}, u32[]{:S(2)}) collective-permute-start(bf16[4,256,256]{2,1,0:T(8,128)(2,1)S(1)} %pad_maximum_fusion.refs_8_), channel_id=1, source_target_pairs={{0,32},{32,64},{64,96},{96,0},{128,224},{160,128},{192,160},{224,1... | collective-permute-start | bytes 1572872 | tf_op jit(solution)/shard_map/ppermute | solution.py:38
  30.0 11.9 %collective-permute-start.7 = (bf16[1024,256]{1,0:T(8,128)(2,1)S(1)}, bf16[1024,256]{1,0:T(8,128)(2,1)S(1)}, u32[]{:S(2)}, u32[]{:S(2)}) collective-permute-start(bf16[1024,256]{1,0:T(8,128)(2,1)S(1)} %collective-permute-done.6.refs_4_), channel_id=1, source_target_pairs={{0,1},{1,2},{2,3},{3,0},{4,5},{5,6},{6,7},{7,4},{8,9},{9,10},{10,1... | collective-permute-start | bytes 1572872 | tf_op jit(solution)/shard_map/ppermute | solution.py:45
  36.3 5.6 %collective-permute-start.10 = (bf16[1024,256]{1,0:T(8,128)(2,1)S(1)}, bf16[1024,256]{1,0:T(8,128)(2,1)S(1)}, u32[]{:S(2)}, u32[]{:S(2)}) collective-permute-start(bf16[1024,256]{1,0:T(8,128)(2,1)S(1)} %collective-permute-done.5.refs_1_), channel_id=1, source_target_pairs={{0,128},{128,0},{1,129},{129,1},{2,130},{130,2},{3,131},{131,3},{4... | collective-permute-start | bytes 1572872 | tf_op jit(solution)/shard_map/ppermute | solution.py:49
  36.3 11.2 %collective-permute-start.9 = (bf16[1024,256]{1,0:T(8,128)(2,1)S(1)}, bf16[1024,256]{1,0:T(8,128)(2,1)S(1)}, u32[]{:S(2)}, u32[]{:S(2)}) collective-permute-start(bf16[1024,256]{1,0:T(8,128)(2,1)S(1)} %collective-permute-done.5.refs_1_), channel_id=1, source_target_pairs={{0,1},{1,2},{2,3},{3,0},{4,5},{5,6},{6,7},{7,4},{8,9},{9,10},{10,1... | collective-permute-start | bytes 1572872 | tf_op jit(solution)/shard_map/ppermute | solution.py:45
  37.7 10.4 %collective-permute-start.14 = (bf16[4,256,256]{2,1,0:T(8,128)(2,1)S(1)}, bf16[4,256,256]{2,1,0:T(8,128)(2,1)S(1)}, u32[]{:S(2)}, u32[]{:S(2)}) collective-permute-start(bf16[4,256,256]{2,1,0:T(8,128)(2,1)S(1)} %collective-permute-done.13.refs_12_), channel_id=1, source_target_pairs={{0,32},{32,64},{64,96},{96,0},{128,224},{160,128},{192,160},{224,1... | collective-permute-start | bytes 1572872 | tf_op jit(solution)/shard_map/ppermute | solution.py:38
  39.2 14.5 %collective-permute-start.16 = (bf16[4,256,256]{2,1,0:T(8,128)(2,1)S(1)}, bf16[4,256,256]{2,1,0:T(8,128)(2,1)S(1)}, u32[]{:S(2)}, u32[]{:S(2)}) collective-permute-start(bf16[4,256,256]{2,1,0:T(8,128)(2,1)S(1)} %collective-permute-done.12.refs_9_), channel_id=1, source_target_pairs={{0,32},{32,64},{64,96},{96,0},{128,224},{160,128},{192,160},{224,1... | collective-permute-start | bytes 1572872 | tf_op jit(solution)/shard_map/ppermute | solution.py:38
  41.9 11.9 %collective-permute-start.17 = (bf16[4,256,256]{2,1,0:T(8,128)(2,1)S(1)}, bf16[4,256,256]{2,1,0:T(8,128)(2,1)S(1)}, u32[]{:S(2)}, u32[]{:S(2)}) collective-permute-start(bf16[4,256,256]{2,1,0:T(8,128)(2,1)S(1)} %collective-permute-done.12.refs_9_), channel_id=1, source_target_pairs={{0,128},{128,0},{1,129},{129,1},{2,130},{130,2},{3,131},{131,3},{4... | collective-permute-start | bytes 1572872 | tf_op jit(solution)/shard_map/ppermute | solution.py:49
  41.9 11.9 %collective-permute-start.8 = (bf16[1024,256]{1,0:T(8,128)(2,1)S(1)}, bf16[1024,256]{1,0:T(8,128)(2,1)S(1)}, u32[]{:S(2)}, u32[]{:S(2)}) collective-permute-start(bf16[1024,256]{1,0:T(8,128)(2,1)S(1)} %collective-permute-done.7.refs_5_), channel_id=1, source_target_pairs={{0,128},{128,0},{1,129},{129,1},{2,130},{130,2},{3,131},{131,3},{4... | collective-permute-start | bytes 1572872 | tf_op jit(solution)/shard_map/ppermute | solution.py:49
  47.5 6.3 %collective-permute-start.11 = (bf16[1024,256]{1,0:T(8,128)(2,1)S(1)}, bf16[1024,256]{1,0:T(8,128)(2,1)S(1)}, u32[]{:S(2)}, u32[]{:S(2)}) collective-permute-start(bf16[1024,256]{1,0:T(8,128)(2,1)S(1)} %collective-permute-done.9.refs_3_), channel_id=1, source_target_pairs={{0,128},{128,0},{1,129},{129,1},{2,130},{130,2},{3,131},{131,3},{4... | collective-permute-start | bytes 1572872 | tf_op jit(solution)/shard_map/ppermute | solution.py:49
  48.1 5.6 %collective-permute-start.15 = (bf16[4,256,256]{2,1,0:T(8,128)(2,1)S(1)}, bf16[4,256,256]{2,1,0:T(8,128)(2,1)S(1)}, u32[]{:S(2)}, u32[]{:S(2)}) collective-permute-start(bf16[4,256,256]{2,1,0:T(8,128)(2,1)S(1)} %collective-permute-done.14.refs_13_), channel_id=1, source_target_pairs={{0,128},{128,0},{1,129},{129,1},{2,130},{130,2},{3,131},{131,3},{4... | collective-permute-start | bytes 1572872 | tf_op jit(solution)/shard_map/ppermute | solution.py:49
  53.7 1.9 %collective-permute-start.18 = (bf16[4,256,256]{2,1,0:T(8,128)(2,1)S(1)}, bf16[4,256,256]{2,1,0:T(8,128)(2,1)S(1)}, u32[]{:S(2)}, u32[]{:S(2)}) collective-permute-start(bf16[4,256,256]{2,1,0:T(8,128)(2,1)S(1)} %collective-permute-done.16.refs_11_), channel_id=1, source_target_pairs={{0,128},{128,0},{1,129},{129,1},{2,130},{130,2},{3,131},{131,3},{4... | collective-permute-start | bytes 1572872 | tf_op jit(solution)/shard_map/ppermute | solution.py:49
  56.4 13.0 %collective-permute-start.23 = (bf16[1024,256]{1,0:T(8,128)(2,1)S(1)}, bf16[1024,256]{1,0:T(8,128)(2,1)S(1)}, u32[]{:S(2)}, u32[]{:S(2)}) collective-permute-start(bf16[1024,256]{1,0:T(8,128)(2,1)S(1)} %products.5), channel_id=1, source_target_pairs={{0,4},{1,5},{2,6},{3,7},{4,8},{5,9},{6,10},{7,11},{8,12},{9,13},{1... | collective-permute-start | bytes 1572872 | tf_op jit(solution)/shard_map/ppermute | solution.py:45
  59.7 15.4 %collective-permute-start.19 = (bf16[1024,256]{1,0:T(8,128)(2,1)S(1)}, bf16[1024,256]{1,0:T(8,128)(2,1)S(1)}, u32[]{:S(2)}, u32[]{:S(2)}) collective-permute-start(bf16[1024,256]{1,0:T(8,128)(2,1)S(1)} %get-tuple-element.16), channel_id=1, source_target_pairs={{0,4},{1,5},{2,6},{3,7},{4,8},{5,9},{6,10},{7,11},{8,12},{9,13},{1... | collective-permute-start | bytes 1572872 | tf_op jit(solution)/shard_map/ppermute | solution.py:45
  69.6 11.1 %collective-permute-start.24 = (bf16[1024,256]{1,0:T(8,128)(2,1)S(1)}, bf16[1024,256]{1,0:T(8,128)(2,1)S(1)}, u32[]{:S(2)}, u32[]{:S(2)}) collective-permute-start(bf16[1024,256]{1,0:T(8,128)(2,1)S(1)} %add_convert_fusion.2), channel_id=1, source_target_pairs={{0,4},{1,5},{2,6},{3,7},{4,8},{5,9},{6,10},{7,11},{8,12},{9,13},{1... | collective-permute-start | bytes 1572872 | tf_op jit(solution)/shard_map/ppermute | solution.py:45
  75.2 11.1 %collective-permute-start.20 = (bf16[1024,256]{1,0:T(8,128)(2,1)S(1)}, bf16[1024,256]{1,0:T(8,128)(2,1)S(1)}, u32[]{:S(2)}, u32[]{:S(2)}) collective-permute-start(bf16[1024,256]{1,0:T(8,128)(2,1)S(1)} %add_convert_fusion.4), channel_id=1, source_target_pairs={{0,4},{1,5},{2,6},{3,7},{4,8},{5,9},{6,10},{7,11},{8,12},{9,13},{1... | collective-permute-start | bytes 1572872 | tf_op jit(solution)/shard_map/ppermute | solution.py:45
  80.8 11.1 %collective-permute-start.25 = (bf16[1024,256]{1,0:T(8,128)(2,1)S(1)}, bf16[1024,256]{1,0:T(8,128)(2,1)S(1)}, u32[]{:S(2)}, u32[]{:S(2)}) collective-permute-start(bf16[1024,256]{1,0:T(8,128)(2,1)S(1)} %add_convert_fusion.1), channel_id=1, source_target_pairs={{0,4},{1,5},{2,6},{3,7},{4,8},{5,9},{6,10},{7,11},{8,12},{9,13},{1... | collective-permute-start | bytes 1572872 | tf_op jit(solution)/shard_map/ppermute | solution.py:45
  86.4 11.2 %collective-permute-start.21 = (bf16[1024,256]{1,0:T(8,128)(2,1)S(1)}, bf16[1024,256]{1,0:T(8,128)(2,1)}, u32[]{:S(2)}, u32[]{:S(2)}) collective-permute-start(bf16[1024,256]{1,0:T(8,128)(2,1)S(1)} %add_convert_fusion.3), channel_id=1, source_target_pairs={{0,4},{1,5},{2,6},{3,7},{4,8},{5,9},{6,10},{7,11},{8,12},{9,13},{1... | collective-permute-start | bytes 1572872 | tf_op jit(solution)/shard_map/ppermute | solution.py:45
  92.1 11.1 %collective-permute-start.26 = (bf16[1024,256]{1,0:T(8,128)(2,1)S(1)}, bf16[1024,256]{1,0:T(8,128)(2,1)S(1)}, u32[]{:S(2)}, u32[]{:S(2)}) collective-permute-start(bf16[1024,256]{1,0:T(8,128)(2,1)S(1)} %add_convert_fusion), channel_id=1, source_target_pairs={{0,4},{1,5},{2,6},{3,7},{4,8},{5,9},{6,10},{7,11},{8,12},{9,13},{1... | collective-permute-start | bytes 1572872 | tf_op jit(solution)/shard_map/ppermute | solution.py:45
  97.6 5.5 %collective-permute-start.22 = (bf16[1024,256]{1,0:T(8,128)(2,1)}, bf16[1024,256]{1,0:T(8,128)(2,1)S(1)}, u32[]{:S(2)}, u32[]{:S(2)}) collective-permute-start(bf16[1024,256]{1,0:T(8,128)(2,1)} %collective-permute-done.21), channel_id=1, source_target_pairs={{0,128},{128,0},{1,129},{129,1},{2,130},{130,2},{3,131},{131,3},{4... | collective-permute-start | bytes 1572872 | tf_op jit(solution)/shard_map/ppermute | solution.py:49
  97.7 2.2 %collective-permute-start.1 = (bf16[128,1024]{1,0:T(8,128)(2,1)S(1)}, bf16[128,1024]{1,0:T(8,128)(2,1)S(1)}, u32[]{:S(2)}, u32[]{:S(2)}) collective-permute-start(bf16[128,1024]{1,0:T(8,128)(2,1)S(1)} %get-tuple-element.27), channel_id=1, source_target_pairs={{0,128},{128,0},{1,129},{129,1},{2,130},{130,2},{3,131},{131,3},{4... | collective-permute-start | bytes 786440 | tf_op jit(solution)/shard_map/ppermute | solution.py:49
